TPU v7x, 32 devices: a whole 2x2x4 slice. The times are simulated.
32 devices in a mesh: tm: 8 (over y, x, core), space: 4 (over z).
Axes of the slice: x: 2, y: 2, z: 4, core: 2. Of those that a mesh axis runs over, the one named last changes fastest.
Arguments:
- c_state: float32 [8, 3, 2, 512, 1024], P('tm', None, None, 'space'), may hold values from -4 to 4
- init: float32 [3, 2, 512, 1024], P(None, None, 'space'), may hold values from -4 to 4
Outputs:
- new_c: float32 [8, 3, 2, 512, 1024], P('tm', None, None, 'space')
- residual: float32 [8, 3, 2, 512, 1024], P('tm', None, None, 'space')
All inputs are finite; a program needn't handle non-finite values.
Results may differ from a plain program's by a relative error of at most 0.00019.
Values sent between devices are 32-bit elements; how exact they have to be, the bound alone decides.
A program may use at most 128 MiB of HBM per device.

v0:
```python
import math

import jax
import jax.numpy as jnp
import numpy as np
from jax import lax
from jax.experimental import pallas as pl
from jax.experimental.pallas import tpu as pltpu
from jax.sharding import Mesh, PartitionSpec as P

CF = 2
CORIOLIS = 1.0
HYPERDIFFUSION = 0.25
COURANT = 0.4
RADIX = 8
ROWS = 32
SLAB = ("ta", "core")
SPACE = "sp"
EVERY = ("ta", "core", "sp")


def split_pair(values):
    high = values.astype(jnp.bfloat16)
    return high, (values - high.astype(jnp.float32)).astype(jnp.bfloat16)


def table_pair(values):
    high = lax.reduce_precision(values, 8, 7)
    return jnp.stack([high, values - high], axis=-3).astype(jnp.bfloat16)


def dot3(left, right):
    def one(a, b):
        return jnp.dot(a, b, preferred_element_type=jnp.float32)

    return one(left[0], right[0]) + (one(left[0], right[1]) + one(left[1], right[0]))


def small_fft(parts, sign):
    count = len(parts)
    if count == 1:
        return parts
    even = small_fft(parts[0::2], sign)
    odd = small_fft(parts[1::2], sign)
    low, high = [], []
    for k in range(count // 2):
        re, im = odd[k]
        if k == 0:
            tr, ti = re, im
        elif 4 * k == count:
            tr, ti = (-im, re) if sign > 0 else (im, -re)
        else:
            c = math.cos(2.0 * math.pi * k / count)
            s = sign * math.sin(2.0 * math.pi * k / count)
            tr, ti = re * c - im * s, re * s + im * c
        low.append((even[k][0] + tr, even[k][1] + ti))
        high.append((even[k][0] - tr, even[k][1] - ti))
    return low + high


def lane_tables(grid_size, sign):
    lanes = grid_size // RADIX
    n = np.arange(lanes)
    angle = 2.0 * np.pi * (n[:, None] * n[None, :] % lanes) / lanes
    c, s = np.cos(angle), sign * np.sin(angle)
    full = jnp.asarray(np.block([[c, s], [-s, c]]), jnp.float32)
    turn = 2.0 * np.pi * (np.arange(RADIX)[:, None] * n[None, :]) / grid_size
    twiddle = np.stack([np.cos(turn), sign * np.sin(turn)]).astype(np.float32)
    return table_pair(full), jnp.asarray(twiddle)


def prop_factors(steps, wave_x, wave_y, grid_size):
    time_step = COURANT / grid_size
    squared = wave_x * wave_x + wave_y * wave_y
    frequency = jnp.sqrt(CORIOLIS * CORIOLIS + squared)
    ratio = squared / (0.25 * grid_size * grid_size)
    log_damp = -HYPERDIFFUSION * (ratio * ratio) * (ratio * ratio)
    phase_angle = frequency * (steps * time_step)
    first_coef = jnp.sin(phase_angle) / frequency
    second_coef = (1.0 - jnp.cos(phase_angle)) / (frequency * frequency)
    damping = jnp.exp(steps * log_damp)
    return first_coef, second_coef, damping


def apply_parts(state, factors, kx, ky):
    first, second, damp = factors
    (xr, xi), (yr, yi), (hr, hi) = state
    done = []
    for x, y, p in ((xr, yr, -hi), (xi, yi, hr)):
        m1 = CORIOLIS * y - kx * p
        m2 = -CORIOLIS * x - ky * p
        m3 = kx * x + ky * y
        n1 = CORIOLIS * m2 - kx * m3
        n2 = -CORIOLIS * m1 - ky * m3
        n3 = kx * m1 + ky * m2
        done.append(
            (
                (x + first * m1 + second * n1) * damp,
                (y + first * m2 + second * n2) * damp,
                (p + first * m3 + second * n3) * damp,
            )
        )
    real, imag = done
    return ((real[0], imag[0]), (real[1], imag[1]), (imag[2], -real[2]))


def apply_array(state, factors, kx, ky):
    fields = tuple((state[f, 0], state[f, 1]) for f in range(3))
    made = apply_parts(fields, factors, kx, ky)
    return jnp.stack([jnp.stack(pair) for pair in made])


def waves_x(grid_size):
    counter = jnp.arange(grid_size, dtype=jnp.int32)
    return jnp.where(counter < grid_size // 2, counter, counter - grid_size).astype(jnp.float32)[None]


def row_tables(grid_size, kept):
    quarter, per = grid_size // 4, grid_size // 8
    y = jnp.arange(quarter, dtype=jnp.int32)
    q = jnp.arange(4, dtype=jnp.int32)
    ky = 4 * jnp.arange(per, dtype=jnp.int32)[None] + q[:, None]

    def waves(turns):
        angle = 2.0 * math.pi / grid_size * (turns % grid_size).astype(jnp.float32)
        return jnp.cos(angle) / grid_size, jnp.sin(angle) / grid_size

    c, s = waves(y[None, :, None] * ky[:, None, :])
    weight = jnp.where(ky == 0, 1.0, 2.0).astype(jnp.float32)[:, None, :]
    c, s = c * weight, s * weight
    inv_even = jnp.stack([jnp.concatenate([c[k], -s[k]], axis=1) for k in (0, 2)])
    inv_odd = jnp.concatenate(
        [
            jnp.concatenate([c[1], -s[1], c[3], -s[3]], axis=1),
            jnp.concatenate([s[1], c[1], -s[3], -c[3]], axis=1),
        ],
        axis=0,
    )
    c, s = waves(ky[:, :kept, None] * y[None, None, :])
    fwd_even = jnp.stack([jnp.concatenate([c[k], -s[k]], axis=0) for k in (0, 2)])
    fwd_odd = jnp.concatenate(
        [
            jnp.concatenate([c[1], -s[1]], axis=1),
            jnp.concatenate([-s[1], -c[1]], axis=1),
            jnp.concatenate([c[3], s[3]], axis=1),
            jnp.concatenate([-s[3], c[3]], axis=1),
        ],
        axis=0,
    )
    return [table_pair(t) for t in (inv_even, inv_odd, fwd_even, fwd_odd)]


def scalars(*values):
    return jnp.stack([jnp.asarray(v, jnp.int32) for v in values])


def whole_smem():
    return pl.BlockSpec(memory_space=pltpu.SMEM)


def deal(c_state, init, last, ident, group):
    _, _, _, rows, grid_size = c_state.shape
    per = rows // 4

    def kernel(at_ref, c_ref, i_ref, *refs):
        outs, held, dealt = refs[:group], refs[group], refs[group + 1]
        tile = held.shape[2]

        @pl.when(at_ref[0] > 0)
        def _():
            for n in range(held.shape[0]):
                held[n] = i_ref[0, 0, :, n * tile : (n + 1) * tile]

        @pl.when(at_ref[0] == 0)
        def _():
            for n in range(held.shape[0]):
                held[n] = c_ref[0, 0, 0, :, n * tile : (n + 1) * tile]

        for q in range(4):
            for n in range(held.shape[0]):
                dealt[q, :, n * tile : (n + 1) * tile] = held[n, pl.ds(q, per, stride=4), :]
        for turn in range(group):
            side = lax.rem(at_ref[1] + group - turn, group) // (group // 2)
            for h in range(2):
                outs[turn][h, 0, 0] = dealt[side + 2 * h]

    return pl.pallas_call(
        kernel,
        grid=(3, 2),
        in_specs=[
            whole_smem(),
            pl.BlockSpec((1, 1, 1, rows, grid_size), lambda f, c: (0, f, c, 0, 0)),
            pl.BlockSpec((1, 1, rows, grid_size), lambda f, c: (f, c, 0, 0)),
        ],
        out_specs=[pl.BlockSpec((2, 1, 1, per, grid_size), lambda f, c: (0, f, c, 0, 0))] * group,
        out_shape=[jax.ShapeDtypeStruct((2, 3, 2, per, grid_size), jnp.float32)] * group,
        scratch_shapes=[
            pltpu.VMEM((grid_size // 128, rows, 128), jnp.float32),
            pltpu.VMEM((4, per, grid_size), jnp.float32),
        ],
        name="deal",
    )(scalars(last, ident), c_state, init)


def fine_steps(landed, factors, tables, grid_size, kept, low):
    group = len(landed)
    _, _, _, short, _ = landed[0].shape
    per = grid_size // 8
    lanes = grid_size // RADIX
    half = RADIX // 2
    blocks = per // ROWS
    limit = float(grid_size // 3)
    zones = -(-(grid_size // 3 + 1) // (4 * short))
    dt = COURANT / grid_size
    inv_even, inv_odd, fwd_even, fwd_odd = tables["rows"]
    inv_x, inv_tw = tables["inv_x"]
    fwd_x, fwd_tw = tables["fwd_x"]

    def kernel(*refs):
        pieces = refs[:group]
        fac, ie, io, fe, fo, ix, itw, fx, ftw, out = refs[group : group + 10]
        state, fields, modes, delta, load, fsend, frecv, msend, mrecv = refs[group + 10 :]
        ta, me, z = (lax.axis_index(name) for name in EVERY)
        mate = (ta, 1 - me, z)
        kx = lax.broadcasted_iota(jnp.int32, (1, grid_size), 1)
        kx = jnp.where(kx < grid_size // 2, kx, kx - grid_size).astype(jnp.float32)
        slots = (2 * me, 2 - me)

        barrier = pltpu.get_barrier_semaphore()
        pl.semaphore_signal(barrier, inc=1, device_id=mate, device_id_type=pl.DeviceIdType.MESH)
        loads = []
        for n in range(group):
            at = lax.rem(n + me * (group // 2), group) * short
            loads.append(
                pltpu.make_async_copy(
                    pieces[n], state.at[:, :, :, pl.ds(pl.multiple_of(at, 8), short)], load.at[n]
                )
            )
            loads[-1].start()
        for copy in loads:
            copy.wait()
        pl.semaphore_wait(barrier, 1)

        def field_copy(b):
            h, at = b // blocks, pl.multiple_of(b % blocks * ROWS, ROWS)
            return pltpu.make_async_remote_copy(
                fields.at[2, :, h, :, pl.ds(at, ROWS)],
                fields.at[me, :, h, :, pl.ds(at, ROWS)],
                fsend.at[b],
                frecv.at[b],
                device_id=mate,
                device_id_type=pl.DeviceIdType.MESH,
            )

        def mode_copy(j):
            return pltpu.make_async_remote_copy(
                modes.at[2, j],
                modes.at[me, j],
                msend.at[j],
                mrecv.at[j],
                device_id=mate,
                device_id_type=pl.DeviceIdType.MESH,
            )

        def rows_ky(h, at, count):
            m = lax.broadcasted_iota(jnp.int32, (count, 1), 0) + at
            return (4 * m + 2 * h + me).astype(jnp.float32)

        def inverse(b, carry):
            h, at = b // blocks, pl.multiple_of(b % blocks * ROWS, ROWS)
            ky = rows_ky(h, at, ROWS)
            row = pl.ds(at, ROWS)
            for f in range(4):
                if f < 3:
                    re, im = state[h, f, 0, row], state[h, f, 1, row]
                else:
                    re = ky * state[h, 0, 1, row] - kx * state[h, 1, 1, row]
                    im = kx * state[h, 1, 0, row] - ky * state[h, 0, 0, row]
                parts = [
                    (re[:, n * lanes : (n + 1) * lanes], im[:, n * lanes : (n + 1) * lanes])
                    for n in range(RADIX)
                ]
                turned = []
                for k, (a, b_) in enumerate(small_fft(parts, 1.0)):
                    if k > 0:
                        c, s = itw[0, k : k + 1], itw[1, k : k + 1]
                        a, b_ = a * c - b_ * s, a * s + b_ * c
                    turned.append(jnp.concatenate([a, b_], axis=1))
                made = dot3(split_pair(jnp.concatenate(turned, axis=0)), (ix[0], ix[1]))
                for k in range(RADIX):
                    for c in range(2):
                        fields[slots[k // half], k % half, h, c, row, f * lanes : (f + 1) * lanes] = made[
                            k * ROWS : (k + 1) * ROWS, c * lanes : (c + 1) * lanes
                        ]
            field_copy(b).start()
            return carry

        def middle(j, carry):
            def rows(c, h):
                return fields[c, j, h].reshape(2 * per, 4 * lanes)

            even = dot3((ie[0, 0], ie[0, 1]), split_pair(rows(0, 0)))
            other = dot3((ie[1, 0], ie[1, 1]), split_pair(rows(0, 1)))
            odd = dot3(
                (io[0], io[1]), split_pair(jnp.concatenate([rows(1, 0), rows(1, 1)], axis=0))
            )
            re, im = odd[: 2 * per], odd[2 * per :]
            plus, minus = even + other, even - other
            made = []
            for grid in (plus + re, minus - im, plus - re, minus + im):
                u, v, h, w = (grid[:, f * lanes : (f + 1) * lanes] for f in range(4))
                made.append(
                    jnp.concatenate([w * v, w * u, 0.5 * (u * u + v * v), h * u, h * v], axis=1)
                )
            a, b = made[0] + made[2], made[1] + made[3]
            for h, term in enumerate((a + b, a - b)):
                got = dot3((fe[h, 0], fe[h, 1]), split_pair(term))
                modes[slots[0], j, h] = got.reshape(2, kept, 5 * lanes)
            term = jnp.concatenate([made[0] - made[2], made[1] - made[3]], axis=0)
            got = dot3((fo[0], fo[1]), split_pair(term))
            for h in range(2):
                modes[slots[1], j, h] = got[2 * kept * h : 2 * kept * (h + 1)].reshape(
                    2, kept, 5 * lanes
                )
            mode_copy(j).start()
            return carry

        def read(ref, at):
            return tuple(
                tuple(
                    jnp.concatenate([ref[h, f, c, pl.ds(at, 8)] for h in range(2)], axis=0)
                    for c in range(2)
                )
                for f in range(3)
            )

        def write(ref, at, values):
            for f in range(3):
                for c in range(2):
                    for h in range(2):
                        ref[h, f, c, pl.ds(at, 8)] = values[f][c][8 * h : 8 * h + 8]

        def rows_of(i):
            at = pl.multiple_of(i * 8, 8)
            ky = jnp.concatenate([rows_ky(h, at, 8) for h in range(2)], axis=0)
            factors = tuple(
                jnp.concatenate([fac[n, h, pl.ds(at, 8)] for h in range(2)], axis=0) for n in range(3)
            )
            return at, ky, factors

        def plain(i, carry):
            at, ky, factors = rows_of(i)
            write(state, at, apply_parts(read(state, at), factors, kx, ky))
            return carry

        def forward(step):
            def body(i, carry):
                at, ky, factors = rows_of(i)

                def piece(f, c, k):
                    return jnp.concatenate(
                        [
                            modes[k // half, k % half, h, c, pl.ds(at, 8), f * lanes : (f + 1) * lanes]
                            for h in range(2)
                        ],
                        axis=0,
                    )

                stacked = jnp.concatenate(
                    [
                        jnp.concatenate([piece(f, 0, k), piece(f, 1, k)], axis=1)
                        for f in range(5)
                        for k in range(RADIX)
                    ],
                    axis=0,
                )
                made = dot3(split_pair(stacked), (fx[0], fx[1]))
                found = []
                for f in range(5):
                    parts = []
                    for k in range(RADIX):
                        start = (f * RADIX + k) * 16
                        a = made[start : start + 16, :lanes]
                        b = made[start : start + 16, lanes:]
                        if k > 0:
                            c, s = ftw[0, k : k + 1], ftw[1, k : k + 1]
                            a, b = a * c - b * s, a * s + b * c
                        parts.append((a, b))
                    parts = small_fft(parts, -1.0)
                    found.append(
                        tuple(jnp.concatenate([p[c] for p in parts], axis=1) for c in range(2))
                    )
                (ar, ai), (br, bi), (kr, ki), (pr, pi), (qr, qi) = found
                inside = (jnp.abs(kx) <= limit) & (ky <= limit)

                def keep(values):
                    return jnp.where(inside, dt * values, 0.0)

                change = (
                    (keep(ar + kx * ki), keep(ai - kx * kr)),
                    (keep(ky * ki - br), -keep(bi + ky * kr)),
                    (keep(kx * pi + ky * qi), -keep(kx * pr + ky * qr)),
                )

                def add(left, right):
                    return tuple(tuple(a + b for a, b in zip(p, q)) for p, q in zip(left, right))

                if step == 0:
                    change = apply_parts(change, factors, kx, ky)
                    write(delta, at, change)
                    moved = apply_parts(read(state, at), factors, kx, ky)
                    write(state, at, add(moved, change))
                else:
                    change = add(change, read(delta, at))
                    change = apply_parts(change, factors, kx, ky)
                    zone = at // short
                    inner = pl.multiple_of(lax.rem(at, short), 8)
                    for f in range(3):
                        for c in range(2):
                            for h in range(2):
                                value = change[f][c][8 * h : 8 * h + 8]
                                out[zone, h, f, c, pl.ds(inner, 8), :low] = value[:, :low]
                                out[zone, h, f, c, pl.ds(inner, 8), low:] = value[:, grid_size - low :]
                return carry

            return body

        for step in range(CF):
            lax.fori_loop(0, 2 * blocks, inverse, 0)
            for b in range(2 * blocks):
                field_copy(b).wait()
            lax.fori_loop(0, half, middle, 0)
            if step < CF - 1:
                lax.fori_loop(kept // 8, per // 8, plain, 0)
            for j in range(half):
                mode_copy(j).wait()
            lax.fori_loop(0, kept // 8, forward(step), 0)
        if kept < zones * short:
            for h in range(2):
                for f in range(3):
                    for c in range(2):
                        start = kept - (zones - 1) * short
                        out[zones - 1, h, f, c, start:] = jnp.zeros((short - start, 2 * low), jnp.float32)

    ops = [factors, inv_even, inv_odd, fwd_even, fwd_odd, inv_x, inv_tw, fwd_x, fwd_tw]
    return pl.pallas_call(
        kernel,
        in_specs=[pl.BlockSpec(memory_space=pl.ANY)] * group
        + [pl.BlockSpec(memory_space=pltpu.VMEM)] * len(ops),
        out_specs=pl.BlockSpec(memory_space=pltpu.VMEM),
        out_shape=jax.ShapeDtypeStruct((zones, 2, 3, 2, short, 2 * low), jnp.float32),
        scratch_shapes=[
            pltpu.VMEM((2, 3, 2, per, grid_size), jnp.float32),
            pltpu.VMEM((3, half, 2, 2, per, 4 * lanes), jnp.float32),
            pltpu.VMEM((3, half, 2, 2, kept, 5 * lanes), jnp.float32),
            pltpu.VMEM((2, 3, 2, kept, grid_size), jnp.float32),
            pltpu.SemaphoreType.DMA((group,)),
            pltpu.SemaphoreType.DMA((2 * blocks,)),
            pltpu.SemaphoreType.DMA((2 * blocks,)),
            pltpu.SemaphoreType.DMA((half,)),
            pltpu.SemaphoreType.DMA((half,)),
        ],
        compiler_params=pltpu.CompilerParams(
            collective_id=0, has_side_effects=True, vmem_limit_bytes=62 * 1024 * 1024
        ),
        name="fine_steps",
    )(*landed, *ops)


def slab_scan(data, factors, kx, ky):
    def kernel(data_ref, fac_ref, kx_ref, ky_ref, out_ref):
        kx, ky = kx_ref[...], ky_ref[...]
        factors = (fac_ref[0], fac_ref[1], fac_ref[2])
        carried = None
        for k in range(data_ref.shape[0]):
            new = tuple((data_ref[k, f, 0], data_ref[k, f, 1]) for f in range(3))
            if carried is not None:
                moved = apply_parts(carried, factors, kx, ky)
                new = tuple((moved[f][0] + new[f][0], moved[f][1] + new[f][1]) for f in range(3))
            for f in range(3):
                for c in range(2):
                    out_ref[k, f, c] = new[f][c]
            carried = new

    slabs, _, _, rows, width = data.shape
    return pl.pallas_call(
        kernel,
        grid=(width // 128,),
        in_specs=[
            pl.BlockSpec((slabs, 3, 2, rows, 128), lambda i: (0, 0, 0, 0, i)),
            pl.BlockSpec((3, rows, 128), lambda i: (0, 0, i)),
            pl.BlockSpec((1, 128), lambda i: (0, i)),
            pl.BlockSpec((rows, 1), lambda i: (0, 0)),
        ],
        out_specs=pl.BlockSpec((slabs, 3, 2, rows, 128), lambda i: (0, 0, 0, 0, i)),
        out_shape=jax.ShapeDtypeStruct(data.shape, jnp.float32),
        name="slab_scan",
    )(data, factors, kx, ky)


def shards(c_state, init):
    rows, grid_size = c_state.shape[3:]
    group = lax.axis_size(SPACE)
    slabs = lax.axis_size(SLAB)
    slab = lax.axis_index(SLAB)
    core = lax.axis_index("core")
    zone = lax.axis_index(SPACE)
    short = rows // 4
    limit = grid_size // 3
    zones = -(-(limit + 1) // rows)
    kept = -(-(limit // 4 + 1) // 8) * 8
    low = (limit // 128 + 1) * 128
    where = (group // 2 - 1, group // 2)

    def device(k, z):
        return k * group + z

    pieces = deal(c_state, init, slab == slabs - 1, zone, group)
    landed = []
    for n, piece in enumerate(pieces):
        links = [
            (device(k, (n + c * (group // 2)) % group), device(k // 2 * 2 + c, where[k % 2]))
            for k in range(slabs)
            for c in range(2)
        ]
        landed.append(lax.ppermute(piece, EVERY, links))
    links = [(device(k, z), device(k + 1, z)) for k in range(slabs - 1) for z in range(group)]
    before = jnp.where(slab == 0, init, lax.ppermute(c_state[0], EVERY, links))

    kx = waves_x(grid_size)
    tables = {
        "rows": row_tables(grid_size, kept),
        "inv_x": lane_tables(grid_size, 1.0),
        "fwd_x": lane_tables(grid_size, -1.0),
    }
    ky = 4 * jnp.arange(grid_size // 8, dtype=jnp.int32)[None] + 2 * jnp.arange(2, dtype=jnp.int32)[:, None]
    ky = (ky + core).astype(jnp.float32)[:, :, None]
    factors = jnp.stack(prop_factors(1.0, kx[None], ky, grid_size))

    ky = (zone * rows + jnp.arange(rows, dtype=jnp.int32)).astype(jnp.float32)[:, None]
    first = apply_array(init, prop_factors((CF * (slab + 1)).astype(jnp.float32), kx, ky, grid_size), kx, ky)
    second = apply_array(before, prop_factors(float(CF), kx, ky, grid_size), kx, ky) - c_state[0]
    landed, factors, tables, first, second = lax.optimization_barrier((landed, factors, tables, first, second))
    made = fine_steps(landed, factors, tables, grid_size, kept, low)

    got = []
    for n in range(zones):
        piece = lax.dynamic_index_in_dim(made, (n + core) % zones, 0, keepdims=False)
        links = [
            (device(k // 2 * 2 + c, where[k % 2]), device((k + 1) % slabs, (n + c) % zones))
            for k in range(slabs)
            for c in range(2)
        ]
        got.append(lax.ppermute(piece, EVERY, links))
    got = jnp.stack(got)
    sides = [lax.dynamic_index_in_dim(got, (zone + zones - c) % zones, 0, keepdims=False) for c in range(2)]
    off = jnp.stack(sides, axis=-3).transpose(1, 2, 4, 0, 3, 5).reshape(3, 2, short, 4, 2 * low)
    off = jnp.where(zone < zones, off.reshape(3, 2, rows, 2 * low), 0.0)

    per = rows // slabs
    kx_low = jnp.concatenate([kx[:, :low], kx[:, grid_size - low :]], axis=1)
    start = zone * rows + slab * per
    ky = (start + jnp.arange(per, dtype=jnp.int32)).astype(jnp.float32)[:, None]
    coarse = jnp.stack(prop_factors(float(CF), kx_low, ky, grid_size))
    split = off.reshape(3, 2, slabs, per, 2 * low).transpose(2, 0, 1, 3, 4)
    split = lax.all_to_all(split, SLAB, split_axis=0, concat_axis=0, tiled=True)
    split = slab_scan(split, coarse, kx_low, ky)
    split = lax.all_to_all(split, SLAB, split_axis=0, concat_axis=0, tiled=True)
    moved = split.transpose(1, 2, 0, 3, 4).reshape(off.shape)

    def widen(base, extra):
        return jnp.concatenate(
            [
                base[..., :low] + extra[..., :low],
                base[..., low : grid_size - low],
                base[..., grid_size - low :] + extra[..., low:],
            ],
            axis=-1,
        )

    return widen(first, moved)[None], widen(second, off)[None]


def solution(mesh):
    slabs, space = mesh.devices.shape
    fine = Mesh(mesh.devices.reshape(slabs // 2, 2, space), EVERY)
    spec = P(SLAB, None, None, SPACE, None)
    return jax.shard_map(
        shards,
        mesh=fine,
        in_specs=(spec, P(None, None, SPACE, None)),
        out_specs=(spec, spec),
        check_vma=False,
    )
```

profile of v0, /device:TPU:0, one launch (start us, length us, event | category | flops | bytes accessed | tf_op | source)
XLA Modules:
  0.0 303.2 jit_solution(10229388748867421146)
XLA Ops:
  0.6 2.6 collective-permute-start.4
  3.2 0.6 pad_add_fusion.at_ref
  3.8 7.1 %deal.1 = (f32[2,3,2,32,1024]{4,3,2,1,0:T(8,128)}, f32[2,3,2,32,1024]{4,3,2,1,0:T(8,128)}, f32[2,3,2,32,1024]{4,3,2,1,0:T(8,128)}, f32[2,3,2,32,1024]{4,3,2,1,0:T(8,128)}) custom-call(s32[2]{0:T(128)} %pad_add_fusion.at_ref, f32[1,3,2,128,1024]{4,3,2,1,0:T(8,128)} %c_ref.1, f32[3,2,128,1024]{3,2,1,0:T(8,128)} %i_ref.1), custom_call_target="tpu_custom_call" | custom-call | tf_op jit(solution)/shard_map/deal/pallas_call | solution.py:187
  10.9 5.5 %collective-permute-start = (f32[2,3,2,32,1024]{4,3,2,1,0:T(8,128)}, f32[2,3,2,32,1024]{4,3,2,1,0:T(8,128)}, u32[]{:S(2)}, u32[]{:S(2)}) collective-permute-start(f32[2,3,2,32,1024]{4,3,2,1,0:T(8,128)} %get-tuple-element.21), channel_id=1, source_target_pairs={{0,1},{2,5},{4,2},{6,6},{8,9},{10,13},{12,10},{14,14},{16,17},{18,... | collective-permute-start | bytes 4718600 | tf_op jit(solution)/shard_map/ppermute | solution.py:526
  16.4 1.8 collective-permute-start.1
  18.2 4.9 %collective-permute-start.2 = (f32[2,3,2,32,1024]{4,3,2,1,0:T(8,128)}, f32[2,3,2,32,1024]{4,3,2,1,0:T(8,128)}, u32[]{:S(2)}, u32[]{:S(2)}) collective-permute-start(f32[2,3,2,32,1024]{4,3,2,1,0:T(8,128)} %get-tuple-element.23), channel_id=1, source_target_pairs={{2,1},{0,5},{6,2},{4,6},{10,9},{8,13},{14,10},{12,14},{18,17},{16,... | collective-permute-start | bytes 4718600 | tf_op jit(solution)/shard_map/ppermute | solution.py:526
  23.1 1.8 collective-permute-start.3
  25.0 1.5 cosine_multiply_fusion.1
  26.5 2.1 cosine_multiply_fusion
  28.6 0.9 fusion.76
  29.5 0.8 slice_bitcast_fusion.5
  30.3 0.7 maximum_bitcast_fusion.10
  31.1 0.8 maximum_bitcast_fusion.11
  31.8 0.7 maximum_bitcast_fusion.12
  32.5 0.7 maximum_bitcast_fusion.13
  33.2 1.1 reduce-precision_convert_fusion.3
  34.3 0.8 pad_maximum_fusion.10.refs_7_
  35.1 0.9 fusion.94
  36.0 1.0 maximum_bitcast_fusion.14
  37.3 0.9 pad_maximum_fusion.8.refs_5_
  38.2 0.9 pad_maximum_fusion.6.refs_8_
  39.2 1.0 fusion.96
  40.4 1.1 pad_maximum_fusion.4.refs_6_
  41.6 4.4 %fusion.3 = (f32[1,2,128,1024]{3,2,1,0:T(8,128)S(1)}, f32[1,2,128,1024]{3,2,1,0:T(8,128)S(1)}, f32[1,2,128,1024]{3,2,1,0:T(8,128)S(1)}) fusion(f32[2,128]{1,0:T(2,128)S(1)} %convert_multiply_fusion, f32[1024]{0:T(1024)S(1)} %fusion.92), kind=kLoop, calls=%fused_computation.26 | loop fusion | flops 2883584 | bytes 3150848 | tf_op jit(solution)/shard_map/div | solution.py:79
  46.0 1.9 pad_maximum_fusion.1.refs_4_
  47.9 1.1 copy-done
  49.1 3.4 %fusion.37 = (f32[1,128,1024]{2,1,0:T(8,128)S(1)}, f32[1,128,1024]{2,1,0:T(8,128)S(1)}, f32[1,128,1024]{2,1,0:T(8,128)S(1)}, f32[1,128,1024]{2,1,0:T(8,128)S(1)}) fusion(f32[3,2,128,1024]{3,2,1,0:T(8,128)S(1)} %copy-done, f32[]{:T(128)S(6)} %convert_element_type.157, f32[1024]{0:T(1024)S(1)} %fusion.90, f32[128]{0:T(128)S(1)} %fusion.93, ...), kind=kLoop, calls=%fused_computation.83 | loop fusion | flops 7864320 | bytes 5252104 | tf_op jit(solution)/shard_map/mul | solution.py:98
  52.5 0.7 broadcast_select_fusion
  53.1 5.3 %fusion.35 = (f32[1,128,1024]{2,1,0:T(8,128)S(1)}, f32[1,128,1024]{2,1,0:T(8,128)S(1)}, f32[1,128,1024]{2,1,0:T(8,128)S(1)}) fusion(f32[3,2,128,1024]{3,2,1,0:T(8,128)S(1)} %copy-done, f32[]{:T(128)S(6)} %convert_element_type.157, f32[128]{0:T(128)S(1)} %add_convert_fusion.1, f32[128]{0:T(128)S(1)} %fusion.93, f32[1024]{0:T(1024)S(1)} %fusion.92, ...), kind=kLoop, calls=%fused_computation.81 | loop fusion | flops 8781824 | bytes 6300680 | tf_op jit(solution)/shard_map/mul | solution.py:99
  58.5 3.6 %fusion.45 = (f32[1,128,1024]{2,1,0:T(8,128)S(1)}, f32[1,128,1024]{2,1,0:T(8,128)S(1)}, f32[1,128,1024]{2,1,0:T(8,128)S(1)}, f32[1,128,1024]{2,1,0:T(8,128)S(1)}, f32[1,128,1024]{2,1,0:T(8,128)S(1)}) fusion(f32[3,2,128,1024]{3,2,1,0:T(8,128)S(1)} %broadcast_select_fusion, f32[1024]{0:T(1024)S(1)} %fusion.90, f32[128]{0:T(128)S(1)} %fusion.93, ...), kind=kLoop, calls=%fused_computation.91 | loop fusion | flops 8912896 | bytes 5776384 | tf_op jit(solution)/shard_map/mul | solution.py:98
  62.6 1.9 pad_maximum_fusion.2
  64.5 1.1 copy-done.3
  65.7 2.6 maximum_subtract_fusion
  68.3 15.3 %collective-permute-done.2.refs_2_ = f32[2,3,2,32,1024]{4,3,2,1,0:T(8,128)} collective-permute-done((f32[2,3,2,32,1024]{4,3,2,1,0:T(8,128)}, f32[2,3,2,32,1024]{4,3,2,1,0:T(8,128)}, u32[]{:S(2)}, u32[]{:S(2)}) %collective-permute-start.2) | collective-permute-done | bytes 1572896 | tf_op jit(solution)/shard_map/ppermute | solution.py:526
  83.6 72.6 %fine_steps.1 = f32[3,2,3,2,32,768]{5,4,3,2,1,0:T(8,128)} custom-call(f32[2,3,2,32,1024]{4,3,2,1,0:T(8,128)} %collective-permute-done.refs_0_, f32[2,3,2,32,1024]{4,3,2,1,0:T(8,128)} %collective-permute-done.1.refs_1_, f32[2,3,2,32,1024]{4,3,2,1,0:T(8,128)} %collective-permute-done.2.refs_2_, f32[2,3,2,32,1024]{4,3,2,1,0:T(8,128)} %collective-permute-done.3.refs_3_, ...), custom_call_target="tpu_custom_call" | custom-call | tf_op jit(solution)/shard_map/fine_steps/pallas_call | solution.py:446
  156.1 3.9 %dynamic-slice_bitcast_fusion.4 = (f32[2,3,2,32,768]{4,3,2,1,0:T(8,128)}, f32[2,3,2,32,768]{4,3,2,1,0:T(8,128)}, f32[2,3,2,32,768]{4,3,2,1,0:T(8,128)}) fusion(f32[3,2,3,2,32,768]{5,4,3,2,1,0:T(8,128)} %fine_steps.1, s32[]{:T(128)S(6)} %select_n.221, s32[]{:T(128)S(6)} %select_n.225, s32[]{:T(128)S(6)} %select_n.223), kind=kLoop, calls=%fused_computation.23 | loop fusion | bytes 7077900 | tf_op jit(solution)/shard_map/jit(dynamic_index_in_dim)/squeeze | solution.py:548
  160.1 1.3 collective-permute-start.5
  161.3 0.7 collective-permute-start.6
  162.1 1.3 collective-permute-start.7
  163.4 30.5 %collective-permute-done.5 = f32[2,3,2,32,768]{4,3,2,1,0:T(8,128)S(1)} collective-permute-done((f32[2,3,2,32,768]{4,3,2,1,0:T(8,128)}, f32[2,3,2,32,768]{4,3,2,1,0:T(8,128)S(1)}, u32[]{:S(2)}, u32[]{:S(2)}) %collective-permute-start.5) | collective-permute-done | bytes 1179680 | tf_op jit(solution)/shard_map/ppermute | solution.py:554
  193.9 26.1 %collective-permute-done.7 = f32[2,3,2,32,768]{4,3,2,1,0:T(8,128)S(1)} collective-permute-done((f32[2,3,2,32,768]{4,3,2,1,0:T(8,128)}, f32[2,3,2,32,768]{4,3,2,1,0:T(8,128)S(1)}, u32[]{:S(2)}, u32[]{:S(2)}) %collective-permute-start.7) | collective-permute-done | bytes 1179680 | tf_op jit(solution)/shard_map/ppermute | solution.py:554
  220.0 0.2 pad_maximum_fusion
  220.3 0.2 dynamic-slice_bitcast_fusion.1
  220.7 1.8 copy.11
  222.5 1.7 copy.22
  224.2 4.4 %all-to-all-start = ((f32[8,3,2,16,768]{4,3,2,1,0:T(8,128)}), f32[8,3,2,16,768]{4,3,2,1,0:T(8,128)}, u32[]{:S(2)}, u32[]{:S(2)}) async-start(f32[8,3,2,16,768]{4,3,2,1,0:T(8,128)} %bitcast.367), calls=%async_computation | async-start | bytes 4718592 | tf_op jit(solution)/shard_map/all_to_all | solution.py:566
  228.7 0.6 pad_maximum_fusion.12.kx_ref
  229.3 0.6 add_convert_fusion.ky_ref
  229.9 0.3 fusion.81
  230.2 0.7 pad_maximum_fusion.11.fac_ref
  230.9 27.2 %all-to-all-done.data_ref = f32[8,3,2,16,768]{4,3,2,1,0:T(8,128)} async-done(((f32[8,3,2,16,768]{4,3,2,1,0:T(8,128)}), f32[8,3,2,16,768]{4,3,2,1,0:T(8,128)}, u32[]{:S(2)}, u32[]{:S(2)}) %all-to-all-start) | async-done | bytes 2359328 | tf_op jit(solution)/shard_map/all_to_all | solution.py:566
  258.0 5.6 %slab_scan.1 = f32[8,3,2,16,768]{4,3,2,1,0:T(8,128)} custom-call(f32[8,3,2,16,768]{4,3,2,1,0:T(8,128)} %all-to-all-done.data_ref, f32[3,16,768]{2,1,0:T(8,128)} %pad_maximum_fusion.11.fac_ref, f32[1,768]{1,0:T(1,128)} %pad_maximum_fusion.12.kx_ref, f32[16,1]{1,0:T(8,128)} %add_convert_fusion.ky_ref), custom_call_target="tpu_custom_call" | custom-call | tf_op jit(solution)/shard_map/slab_scan/pallas_call | solution.py:486
  263.6 4.4 %all-to-all-start.1 = ((f32[8,3,2,16,768]{4,3,2,1,0:T(8,128)}), f32[8,3,2,16,768]{4,3,2,1,0:T(8,128)}, u32[]{:S(2)}, u32[]{:S(2)}) async-start(f32[8,3,2,16,768]{4,3,2,1,0:T(8,128)} %slab_scan.1), calls=%async_computation.1 | async-start | bytes 4718592 | tf_op jit(solution)/shard_map/all_to_all | solution.py:568
  268.0 0.8 fusion.98
  268.8 1.1 copy-done.2
  269.9 0.3 copy_add_fusion.1
  270.2 0.8 slice-done.1
  271.0 2.1 maximum_bitcast_fusion.1
  273.1 24.3 %all-to-all-done.1 = f32[8,3,2,16,768]{4,3,2,1,0:T(8,128)} async-done(((f32[8,3,2,16,768]{4,3,2,1,0:T(8,128)}), f32[8,3,2,16,768]{4,3,2,1,0:T(8,128)}, u32[]{:S(2)}, u32[]{:S(2)}) %all-to-all-start.1) | async-done | bytes 2359328 | tf_op jit(solution)/shard_map/all_to_all | solution.py:568
  297.4 2.0 copy.13
  299.4 0.6 copy-done.1
  300.0 0.4 slice_add_fusion.1
  300.4 0.8 slice-done
  301.1 2.1 maximum_bitcast_fusion
  (55 shorter events, 1.4 us)
Async XLA Ops:
  0.6 51.8 %collective-permute-start.4 = (f32[3,2,128,1024]{3,2,1,0:T(8,128)}, f32[3,2,128,1024]{3,2,1,0:T(8,128)S(1)}, u32[]{:S(2)}, u32[]{:S(2)}) collective-permute-start(f32[3,2,128,1024]{3,2,1,0:T(8,128)} %bitcast.365), channel_id=1, source_target_pairs={{0,4},{1,5},{2,6},{3,7},{4,8},{5,9},{6,10},{7,11},{8,12},{9,13},{1... | collective-permute-start | bytes 9437192 | tf_op jit(solution)/shard_map/ppermute | solution.py:528
  10.9 57.4 %collective-permute-start = (f32[2,3,2,32,1024]{4,3,2,1,0:T(8,128)}, f32[2,3,2,32,1024]{4,3,2,1,0:T(8,128)}, u32[]{:S(2)}, u32[]{:S(2)}) collective-permute-start(f32[2,3,2,32,1024]{4,3,2,1,0:T(8,128)} %get-tuple-element.21), channel_id=1, source_target_pairs={{0,1},{2,5},{4,2},{6,6},{8,9},{10,13},{12,10},{14,14},{16,17},{18,... | collective-permute-start | bytes 4718600 | tf_op jit(solution)/shard_map/ppermute | solution.py:526
  16.4 51.9 %collective-permute-start.1 = (f32[2,3,2,32,1024]{4,3,2,1,0:T(8,128)}, f32[2,3,2,32,1024]{4,3,2,1,0:T(8,128)}, u32[]{:S(2)}, u32[]{:S(2)}) collective-permute-start(f32[2,3,2,32,1024]{4,3,2,1,0:T(8,128)} %get-tuple-element.22), channel_id=1, source_target_pairs={{1,1},{3,5},{5,2},{7,6},{9,9},{11,13},{13,10},{15,14},{17,17},{19,... | collective-permute-start | bytes 4718600 | tf_op jit(solution)/shard_map/ppermute | solution.py:526
  18.2 65.4 %collective-permute-start.2 = (f32[2,3,2,32,1024]{4,3,2,1,0:T(8,128)}, f32[2,3,2,32,1024]{4,3,2,1,0:T(8,128)}, u32[]{:S(2)}, u32[]{:S(2)}) collective-permute-start(f32[2,3,2,32,1024]{4,3,2,1,0:T(8,128)} %get-tuple-element.23), channel_id=1, source_target_pairs={{2,1},{0,5},{6,2},{4,6},{10,9},{8,13},{14,10},{12,14},{18,17},{16,... | collective-permute-start | bytes 4718600 | tf_op jit(solution)/shard_map/ppermute | solution.py:526
  23.1 60.4 %collective-permute-start.3 = (f32[2,3,2,32,1024]{4,3,2,1,0:T(8,128)}, f32[2,3,2,32,1024]{4,3,2,1,0:T(8,128)}, u32[]{:S(2)}, u32[]{:S(2)}) collective-permute-start(f32[2,3,2,32,1024]{4,3,2,1,0:T(8,128)} %get-tuple-element.24), channel_id=1, source_target_pairs={{3,1},{1,5},{7,2},{5,6},{11,9},{9,13},{15,10},{13,14},{19,17},{17,... | collective-permute-start | bytes 4718600 | tf_op jit(solution)/shard_map/ppermute | solution.py:526
  26.5 2.1 copy-start.6
  28.6 3.9 %copy-start.4 = (f32[4,256,128]{2,1,0:T(8,128)}, f32[4,256,128]{2,1,0:T(8,128)S(1)}, u32[]{:S(2)}) copy-start(f32[4,256,128]{2,1,0:T(8,128)S(1)} %get-tuple-element.103) | copy-start | bytes 1572868
  28.6 3.9 %copy-start.5 = (f32[4,256,128]{2,1,0:T(8,128)}, f32[4,256,128]{2,1,0:T(8,128)S(1)}, u32[]{:S(2)}) copy-start(f32[4,256,128]{2,1,0:T(8,128)S(1)} %get-tuple-element.104) | copy-start | bytes 1572868
  33.2 3.9 %copy-start.13 = (f32[88,256]{1,0:T(8,128)S(1)}, f32[88,256]{1,0:T(8,128)}, u32[]{:S(2)}) copy-start(f32[88,256]{1,0:T(8,128)} %get-tuple-element.83) | copy-start | bytes 270340
  33.2 3.9 %copy-start.14 = (f32[88,256]{1,0:T(8,128)S(1)}, f32[88,256]{1,0:T(8,128)}, u32[]{:S(2)}) copy-start(f32[88,256]{1,0:T(8,128)} %get-tuple-element.115) | copy-start | bytes 270340
  33.2 3.9 %copy-start.7 = (f32[1,1,256,256]{3,2,1,0:T(8,128)S(1)}, f32[1,1,256,256]{3,2,1,0:T(8,128)}, u32[]{:S(2)}) copy-start(f32[1,1,256,256]{3,2,1,0:T(8,128)} %maximum_bitcast_fusion.10) | copy-start | bytes 786436
  33.2 3.9 %copy-start.8 = (f32[1,1,256,256]{3,2,1,0:T(8,128)S(1)}, f32[1,1,256,256]{3,2,1,0:T(8,128)}, u32[]{:S(2)}) copy-start(f32[1,1,256,256]{3,2,1,0:T(8,128)} %maximum_bitcast_fusion.11) | copy-start | bytes 786436
  37.2 2.9 copy-start.9
  37.2 2.9 copy-start.10
  37.2 2.9 copy-start.11
  37.3 2.9 copy-start.12
  46.0 3.0 copy-start
  62.6 3.0 copy-start.3
  160.1 33.9 %collective-permute-start.5 = (f32[2,3,2,32,768]{4,3,2,1,0:T(8,128)}, f32[2,3,2,32,768]{4,3,2,1,0:T(8,128)S(1)}, u32[]{:S(2)}, u32[]{:S(2)}) collective-permute-start(f32[2,3,2,32,768]{4,3,2,1,0:T(8,128)} %get-tuple-element.46), channel_id=1, source_target_pairs={{1,4},{5,5},{2,8},{6,9},{9,12},{13,13},{10,16},{14,17},{17,20},{21... | collective-permute-start | bytes 3538952 | tf_op jit(solution)/shard_map/ppermute | solution.py:554
  161.3 32.6 %collective-permute-start.6 = (f32[2,3,2,32,768]{4,3,2,1,0:T(8,128)}, f32[2,3,2,32,768]{4,3,2,1,0:T(8,128)S(1)}, u32[]{:S(2)}, u32[]{:S(2)}) collective-permute-start(f32[2,3,2,32,768]{4,3,2,1,0:T(8,128)} %get-tuple-element.48), channel_id=1, source_target_pairs={{1,5},{5,6},{2,9},{6,10},{9,13},{13,14},{10,17},{14,18},{17,21},{2... | collective-permute-start | bytes 3538952 | tf_op jit(solution)/shard_map/ppermute | solution.py:554
  162.1 57.9 %collective-permute-start.7 = (f32[2,3,2,32,768]{4,3,2,1,0:T(8,128)}, f32[2,3,2,32,768]{4,3,2,1,0:T(8,128)S(1)}, u32[]{:S(2)}, u32[]{:S(2)}) collective-permute-start(f32[2,3,2,32,768]{4,3,2,1,0:T(8,128)} %get-tuple-element.47), channel_id=1, source_target_pairs={{1,6},{5,4},{2,10},{6,8},{9,14},{13,12},{10,18},{14,16},{17,22},{2... | collective-permute-start | bytes 3538952 | tf_op jit(solution)/shard_map/ppermute | solution.py:554
  224.2 33.8 %all-to-all-start = ((f32[8,3,2,16,768]{4,3,2,1,0:T(8,128)}), f32[8,3,2,16,768]{4,3,2,1,0:T(8,128)}, u32[]{:S(2)}, u32[]{:S(2)}) async-start(f32[8,3,2,16,768]{4,3,2,1,0:T(8,128)} %bitcast.367), calls=%async_computation | async-start | bytes 4718592 | tf_op jit(solution)/shard_map/all_to_all | solution.py:566
  263.6 33.8 %all-to-all-start.1 = ((f32[8,3,2,16,768]{4,3,2,1,0:T(8,128)}), f32[8,3,2,16,768]{4,3,2,1,0:T(8,128)}, u32[]{:S(2)}, u32[]{:S(2)}) async-start(f32[8,3,2,16,768]{4,3,2,1,0:T(8,128)} %slab_scan.1), calls=%async_computation.1 | async-start | bytes 4718592 | tf_op jit(solution)/shard_map/all_to_all | solution.py:568
  268.0 1.9 copy-start.2
  269.9 1.1 slice-start.1
  297.4 2.6 copy-start.1
  300.0 1.1 slice-start
where the time goes:
time: 305 us; the launch traced here: 303 us
  waiting for transfers between devices  123 us (40%)
  Pallas kernels  85.2 us (28%)
  other arithmetic  48.7 us (16%)
  starting transfers between devices  28.7 us (9%)
  local copies, waits for them, and re-layouts  16.1 us (5%)
    pallas_call x1, Pallas kernels, fine_steps(): pl.pallas_call(kernel, in_specs=[pl.BlockSpec(memory_space=pl.ANY)] * gro...  72.6 us
    ppermute x3, waiting for transfers between devices, shards(): got.append(lax.ppermute(piece, EVERY, links))  56.6 us
    all_to_all x2, waiting for transfers between devices, shards(): split = lax.all_to_all(split, SLAB, split_axis=0, concat_axis=0, tiled=True)  51.5 us
    ppermute x4, waiting for transfers between devices, shards(): landed.append(lax.ppermute(piece, EVERY, links))  15.3 us
    ppermute x4, starting transfers between devices, shards(): landed.append(lax.ppermute(piece, EVERY, links))  14 us
    all_to_all x2, starting transfers between devices, shards(): split = lax.all_to_all(split, SLAB, split_axis=0, concat_axis=0, tiled=True)  8.75 us
    pallas_call x1, Pallas kernels, deal(): pl.pallas_call(kernel, grid=(3, 2), in_specs=[whole_smem(), pl.BlockSpec(...  7.07 us
    mul x2, other arithmetic, apply_parts(): (x + first * m1 + second * n1) * damp  6.98 us
  transfers between devices with their start and end apart: 10, of which 5 were waited for; matrix products, arithmetic and copies ran while one was open for 15% of the time, Pallas kernels for 2%

commit v1 on v0

--- a/solution.py
+++ b/solution.py
@@ -202,8 +202,10 @@
     )(scalars(last, ident), c_state, init)
 
 
-def fine_steps(landed, factors, tables, grid_size, kept, low):
+def fine_steps(landed, factors, scan_factors, tables, grid_size, kept, low, slabs, where):
     group = len(landed)
+    chips = slabs // 2
+    MESH = pl.DeviceIdType.MESH
     _, _, _, short, _ = landed[0].shape
     per = grid_size // 8
     lanes = grid_size // RADIX
@@ -212,22 +214,49 @@
     limit = float(grid_size // 3)
     zones = -(-(grid_size // 3 + 1) // (4 * short))
     dt = COURANT / grid_size
+    total = kept // 8
+    each = short // 8
     inv_even, inv_odd, fwd_even, fwd_odd = tables["rows"]
     inv_x, inv_tw = tables["inv_x"]
     fwd_x, fwd_tw = tables["fwd_x"]
 
     def kernel(*refs):
         pieces = refs[:group]
-        fac, ie, io, fe, fo, ix, itw, fx, ftw, out = refs[group : group + 10]
-        state, fields, modes, delta, load, fsend, frecv, msend, mrecv = refs[group + 10 :]
+        fac, sfac, ie, io, fe, fo, ix, itw, fx, ftw, off_out, sum_out = refs[group : group + 12]
+        state, fields, modes, delta, sent, off, mates, carry_in, sums = refs[group + 12 : group + 21]
+        load, fsend, frecv, msend, mrecv, bsend, brecv, psend, precv, csend, crecv, ssend, srecv, osem, usem = refs[
+            group + 21 :
+        ]
         ta, me, z = (lax.axis_index(name) for name in EVERY)
         mate = (ta, 1 - me, z)
+        is_job = (z == where[0]) | (z == where[1])
+        is_home = z < zones
+        first = ta == 0
+        passes_on = (me == 1) & (ta < chips - 1) & is_home
+        slab = 2 * ta + jnp.where(z == where[1], 1, 0)
+        target = lax.rem(slab + 1, slabs)
+        own = 2 * ta + me
+        source = lax.rem(own + slabs - 1, slabs)
+        source_z = jnp.where(lax.rem(source, 2) == 1, where[1], where[0])
+        home_is_own = (target == own) & is_job & is_home
         kx = lax.broadcasted_iota(jnp.int32, (1, grid_size), 1)
         kx = jnp.where(kx < grid_size // 2, kx, kx - grid_size).astype(jnp.float32)
         slots = (2 * me, 2 - me)
 
         barrier = pltpu.get_barrier_semaphore()
-        pl.semaphore_signal(barrier, inc=1, device_id=mate, device_id_type=pl.DeviceIdType.MESH)
+        pl.semaphore_signal(barrier, inc=1, device_id=mate, device_id_type=MESH)
+        for side in range(2):
+            job = (source // 2, side, source_z)
+            is_self = (source // 2 == ta) & (source_z == z) & (me == side)
+
+            @pl.when(is_home & jnp.logical_not(is_self))
+            def _():
+                pl.semaphore_signal(barrier, inc=1, device_id=job, device_id_type=MESH)
+
+        @pl.when(is_home & (me == 1) & (ta > 0))
+        def _():
+            pl.semaphore_signal(barrier, inc=1, device_id=(ta - 1, me, z), device_id_type=MESH)
+
         loads = []
         for n in range(group):
             at = lax.rem(n + me * (group // 2), group) * short
@@ -239,7 +268,21 @@
             loads[-1].start()
         for copy in loads:
             copy.wait()
-        pl.semaphore_wait(barrier, 1)
+        expected = 1 + jnp.where(is_job, zones, 0) - jnp.where(home_is_own, 1, 0) + jnp.where(passes_on, 1, 0)
+        pl.semaphore_wait(barrier, expected)
+
+        def back_copy(i):
+            return pltpu.make_async_remote_copy(
+                sent.at[i],
+                off.at[me, lax.rem(i, each)],
+                bsend.at[i],
+                brecv.at[me, lax.rem(i, each)],
+                device_id=(target // 2, lax.rem(target, 2), i // each),
+                device_id_type=MESH,
+            )
+
+        def stays(i):
+            return home_is_own & (i // each == z)
 
         def field_copy(b):
             h, at = b // blocks, pl.multiple_of(b % blocks * ROWS, ROWS)
@@ -413,14 +456,22 @@
                 else:
                     change = add(change, read(delta, at))
                     change = apply_parts(change, factors, kx, ky)
-                    zone = at // short
-                    inner = pl.multiple_of(lax.rem(at, short), 8)
                     for f in range(3):
                         for c in range(2):
                             for h in range(2):
                                 value = change[f][c][8 * h : 8 * h + 8]
-                                out[zone, h, f, c, pl.ds(inner, 8), :low] = value[:, :low]
-                                out[zone, h, f, c, pl.ds(inner, 8), low:] = value[:, grid_size - low :]
+                                sent[i, h, f, c, :, :low] = value[:, :low]
+                                sent[i, h, f, c, :, low:] = value[:, grid_size - low :]
+
+                    @pl.when(stays(i))
+                    def _():
+                        at = lax.rem(i, each)
+                        pltpu.make_async_copy(sent.at[i], off.at[me, at], brecv.at[me, at]).start()
+
+                    @pl.when(is_job & jnp.logical_not(stays(i)))
+                    def _():
+                        back_copy(i).start()
+
                 return carry
 
             return body
@@ -435,30 +486,179 @@
             for j in range(half):
                 mode_copy(j).wait()
             lax.fori_loop(0, kept // 8, forward(step), 0)
-        if kept < zones * short:
-            for h in range(2):
-                for f in range(3):
-                    for c in range(2):
-                        start = kept - (zones - 1) * short
-                        out[zones - 1, h, f, c, start:] = jnp.zeros((short - start, 2 * low), jnp.float32)
-
-    ops = [factors, inv_even, inv_odd, fwd_even, fwd_odd, inv_x, inv_tw, fwd_x, fwd_tw]
+
+        kx_low = jnp.concatenate([kx[:, :low], kx[:, grid_size - low :]], axis=1)
+
+        def chunk(ref, side, at):
+            return tuple(
+                tuple(jnp.concatenate([ref[side, at, h, f, c] for h in range(2)], axis=0) for c in range(2))
+                for f in range(3)
+            )
+
+        def moved(n, values, side, at):
+            m = lax.broadcasted_iota(jnp.int32, (8, 1), 0) + (z * short + at * 8)
+            ky = jnp.concatenate([4 * m + 2 * h + side for h in range(2)], axis=0).astype(jnp.float32)
+            factors = tuple(
+                jnp.concatenate([sfac[n, k, side, at, h] for h in range(2)], axis=0) for k in range(3)
+            )
+            return apply_parts(values, factors, kx_low, ky)
+
+        def put(side, at, values):
+            for f in range(3):
+                for c in range(2):
+                    for h in range(2):
+                        sums[side, at, h, f, c] = values[f][c][8 * h : 8 * h + 8]
+            pltpu.make_async_copy(sums.at[side, at], sum_out.at[side, at], usem.at[side, at]).start()
+
+        def plus(left, right):
+            return tuple(tuple(a + b for a, b in zip(p, q)) for p, q in zip(left, right))
+
+        def landed_copy(side, at):
+            return pltpu.make_async_copy(off.at[side, at], off.at[side, at], brecv.at[side, at])
+
+        def off_copy(side, at):
+            return pltpu.make_async_copy(off.at[side, at], off_out.at[side, at], osem.at[side, at])
+
+        def pair_copy(side, at):
+            return pltpu.make_async_remote_copy(
+                off.at[side, at],
+                mates.at[side, at],
+                psend.at[side, at],
+                precv.at[side, at],
+                device_id=(ta, 1, z),
+                device_id_type=MESH,
+            )
+
+        def share_copy(side, at):
+            return pltpu.make_async_remote_copy(
+                carry_in.at[side, at],
+                carry_in.at[side, at],
+                csend.at[side, at],
+                crecv.at[side, at],
+                device_id=(ta, 0, z),
+                device_id_type=MESH,
+            )
+
+        def chain_copy(side, at):
+            return pltpu.make_async_remote_copy(
+                sums.at[side, at],
+                carry_in.at[side, at],
+                ssend.at[side, at],
+                crecv.at[side, at],
+                device_id=(lax.rem(ta + 1, chips), 1, z),
+                device_id_type=MESH,
+            )
+
+        mine = jnp.minimum(each, total - z * each) * 2
+
+        def over(body):
+            def step(t, carry):
+                body(lax.rem(t, 2), t // 2)
+                return carry
+
+            lax.fori_loop(0, mine, step, 0)
+
+        @pl.when(is_home & (me == 0))
+        def _():
+            def start(side, at):
+                landed_copy(side, at).wait()
+                pair_copy(side, at).start()
+                off_copy(side, at).start()
+
+            over(start)
+
+            def rest(side, at):
+                @pl.when(first)
+                def _():
+                    put(side, at, chunk(off, side, at))
+
+                @pl.when(ta > 0)
+                def _():
+                    share_copy(side, at).wait_recv()
+                    put(side, at, plus(chunk(off, side, at), moved(0, chunk(carry_in, side, at), side, at)))
+
+            over(rest)
+
+            def end(side, at):
+                pair_copy(side, at).wait_send()
+
+            over(end)
+
+        @pl.when(is_home & (me == 1))
+        def _():
+            def step(side, at):
+                landed_copy(side, at).wait()
+                off_copy(side, at).start()
+                pair_copy(side, at).wait_recv()
+                both = plus(chunk(off, side, at), moved(0, chunk(mates, side, at), side, at))
+
+                @pl.when(first)
+                def _():
+                    put(side, at, both)
+
+                @pl.when(ta > 0)
+                def _():
+                    chain_copy(side, at).wait_recv()
+                    share_copy(side, at).start()
+                    put(side, at, plus(both, moved(1, chunk(carry_in, side, at), side, at)))
+
+                @pl.when(passes_on)
+                def _():
+                    chain_copy(side, at).start()
+
+            over(step)
+
+            def end(side, at):
+                @pl.when(ta > 0)
+                def _():
+                    share_copy(side, at).wait_send()
+
+                @pl.when(passes_on)
+                def _():
+                    chain_copy(side, at).wait_send()
+
+            over(end)
+
+        @pl.when(is_home)
+        def _():
+            def end(side, at):
+                off_copy(side, at).wait()
+                pltpu.make_async_copy(sums.at[side, at], sum_out.at[side, at], usem.at[side, at]).wait()
+
+            over(end)
+
+        @pl.when(is_job)
+        def _():
+            def end(i, carry):
+                @pl.when(jnp.logical_not(stays(i)))
+                def _():
+                    back_copy(i).wait_send()
+
+                return carry
+
+            lax.fori_loop(0, total, end, 0)
+
+    ops = [factors, scan_factors, inv_even, inv_odd, fwd_even, fwd_odd, inv_x, inv_tw, fwd_x, fwd_tw]
     return pl.pallas_call(
         kernel,
         in_specs=[pl.BlockSpec(memory_space=pl.ANY)] * group
         + [pl.BlockSpec(memory_space=pltpu.VMEM)] * len(ops),
-        out_specs=pl.BlockSpec(memory_space=pltpu.VMEM),
-        out_shape=jax.ShapeDtypeStruct((zones, 2, 3, 2, short, 2 * low), jnp.float32),
+        out_specs=[pl.BlockSpec(memory_space=pl.ANY)] * 2,
+        out_shape=[jax.ShapeDtypeStruct((2, each, 2, 3, 2, 8, 2 * low), jnp.float32)] * 2,
         scratch_shapes=[
             pltpu.VMEM((2, 3, 2, per, grid_size), jnp.float32),
             pltpu.VMEM((3, half, 2, 2, per, 4 * lanes), jnp.float32),
             pltpu.VMEM((3, half, 2, 2, kept, 5 * lanes), jnp.float32),
             pltpu.VMEM((2, 3, 2, kept, grid_size), jnp.float32),
+            pltpu.VMEM((total, 2, 3, 2, 8, 2 * low), jnp.float32),
+            *[pltpu.VMEM((2, each, 2, 3, 2, 8, 2 * low), jnp.float32)] * 4,
             pltpu.SemaphoreType.DMA((group,)),
             pltpu.SemaphoreType.DMA((2 * blocks,)),
             pltpu.SemaphoreType.DMA((2 * blocks,)),
             pltpu.SemaphoreType.DMA((half,)),
             pltpu.SemaphoreType.DMA((half,)),
+            pltpu.SemaphoreType.DMA((total,)),
+            *[pltpu.SemaphoreType.DMA((2, each))] * 9,
         ],
         compiler_params=pltpu.CompilerParams(
             collective_id=0, has_side_effects=True, vmem_limit_bytes=62 * 1024 * 1024
@@ -467,35 +667,41 @@
     )(*landed, *ops)
 
 
-def slab_scan(data, factors, kx, ky):
-    def kernel(data_ref, fac_ref, kx_ref, ky_ref, out_ref):
-        kx, ky = kx_ref[...], ky_ref[...]
-        factors = (fac_ref[0], fac_ref[1], fac_ref[2])
-        carried = None
-        for k in range(data_ref.shape[0]):
-            new = tuple((data_ref[k, f, 0], data_ref[k, f, 1]) for f in range(3))
-            if carried is not None:
-                moved = apply_parts(carried, factors, kx, ky)
-                new = tuple((moved[f][0] + new[f][0], moved[f][1] + new[f][1]) for f in range(3))
-            for f in range(3):
-                for c in range(2):
-                    out_ref[k, f, c] = new[f][c]
-            carried = new
-
-    slabs, _, _, rows, width = data.shape
+def finish(first, second, sums, off, zone, low):
+    _, _, rows, grid_size = first.shape
+    each = sums.shape[1]
+    short = rows // 4
+    limit = grid_size // 3
+
+    def kernel(at_ref, first_ref, second_ref, sum_ref, off_ref, new_ref, res_ref, held):
+        ky = lax.broadcasted_iota(jnp.int32, (rows, 1), 0) + at_ref[0] * rows
+        inside = ky <= limit
+        for base, extra, out in ((first_ref, sum_ref, new_ref), (second_ref, off_ref, res_ref)):
+            for n in range(held.shape[0]):
+                for side in range(2):
+                    for h in range(2):
+                        values = extra[side, :, h, 0, 0, :, n * 128 : (n + 1) * 128]
+                        held[n, pl.ds(side + 2 * h, short, stride=4), :] = values.reshape(short, 128)
+            for n in range(held.shape[0]):
+                at = n * 128 if n * 128 < low else grid_size - 2 * low + n * 128
+                lane = slice(at, at + 128)
+                out[0, 0, 0, :, lane] = base[0, 0, :, lane] + jnp.where(inside, held[n], 0.0)
+            if low * 2 < grid_size:
+                lane = slice(low, grid_size - low)
+                out[0, 0, 0, :, lane] = base[0, 0, :, lane]
+
+    whole = pl.BlockSpec((1, 1, rows, grid_size), lambda f, c: (f, c, 0, 0))
+    extra = pl.BlockSpec((2, each, 2, 1, 1, 8, 2 * low), lambda f, c: (0, 0, 0, f, c, 0, 0))
+    out = pl.BlockSpec((1, 1, 1, rows, grid_size), lambda f, c: (0, f, c, 0, 0))
     return pl.pallas_call(
         kernel,
-        grid=(width // 128,),
-        in_specs=[
-            pl.BlockSpec((slabs, 3, 2, rows, 128), lambda i: (0, 0, 0, 0, i)),
-            pl.BlockSpec((3, rows, 128), lambda i: (0, 0, i)),
-            pl.BlockSpec((1, 128), lambda i: (0, i)),
-            pl.BlockSpec((rows, 1), lambda i: (0, 0)),
-        ],
-        out_specs=pl.BlockSpec((slabs, 3, 2, rows, 128), lambda i: (0, 0, 0, 0, i)),
-        out_shape=jax.ShapeDtypeStruct(data.shape, jnp.float32),
-        name="slab_scan",
-    )(data, factors, kx, ky)
+        grid=(3, 2),
+        in_specs=[whole_smem(), whole, whole, extra, extra],
+        out_specs=[out, out],
+        out_shape=[jax.ShapeDtypeStruct((1, *first.shape), jnp.float32)] * 2,
+        scratch_shapes=[pltpu.VMEM((2 * low // 128, rows, 128), jnp.float32)],
+        name="finish",
+    )(scalars(zone), first, second, sums, off)
 
 
 def shards(c_state, init):
@@ -507,7 +713,6 @@
     zone = lax.axis_index(SPACE)
     short = rows // 4
     limit = grid_size // 3
-    zones = -(-(limit + 1) // rows)
     kept = -(-(limit // 4 + 1) // 8) * 8
     low = (limit // 128 + 1) * 128
     where = (group // 2 - 1, group // 2)
@@ -540,45 +745,19 @@
     ky = (zone * rows + jnp.arange(rows, dtype=jnp.int32)).astype(jnp.float32)[:, None]
     first = apply_array(init, prop_factors((CF * (slab + 1)).astype(jnp.float32), kx, ky, grid_size), kx, ky)
     second = apply_array(before, prop_factors(float(CF), kx, ky, grid_size), kx, ky) - c_state[0]
-    landed, factors, tables, first, second = lax.optimization_barrier((landed, factors, tables, first, second))
-    made = fine_steps(landed, factors, tables, grid_size, kept, low)
-
-    got = []
-    for n in range(zones):
-        piece = lax.dynamic_index_in_dim(made, (n + core) % zones, 0, keepdims=False)
-        links = [
-            (device(k // 2 * 2 + c, where[k % 2]), device((k + 1) % slabs, (n + c) % zones))
-            for k in range(slabs)
-            for c in range(2)
-        ]
-        got.append(lax.ppermute(piece, EVERY, links))
-    got = jnp.stack(got)
-    sides = [lax.dynamic_index_in_dim(got, (zone + zones - c) % zones, 0, keepdims=False) for c in range(2)]
-    off = jnp.stack(sides, axis=-3).transpose(1, 2, 4, 0, 3, 5).reshape(3, 2, short, 4, 2 * low)
-    off = jnp.where(zone < zones, off.reshape(3, 2, rows, 2 * low), 0.0)
-
-    per = rows // slabs
     kx_low = jnp.concatenate([kx[:, :low], kx[:, grid_size - low :]], axis=1)
-    start = zone * rows + slab * per
-    ky = (start + jnp.arange(per, dtype=jnp.int32)).astype(jnp.float32)[:, None]
-    coarse = jnp.stack(prop_factors(float(CF), kx_low, ky, grid_size))
-    split = off.reshape(3, 2, slabs, per, 2 * low).transpose(2, 0, 1, 3, 4)
-    split = lax.all_to_all(split, SLAB, split_axis=0, concat_axis=0, tiled=True)
-    split = slab_scan(split, coarse, kx_low, ky)
-    split = lax.all_to_all(split, SLAB, split_axis=0, concat_axis=0, tiled=True)
-    moved = split.transpose(1, 2, 0, 3, 4).reshape(off.shape)
-
-    def widen(base, extra):
-        return jnp.concatenate(
-            [
-                base[..., :low] + extra[..., :low],
-                base[..., low : grid_size - low],
-                base[..., grid_size - low :] + extra[..., low:],
-            ],
-            axis=-1,
-        )
-
-    return widen(first, moved)[None], widen(second, off)[None]
+    side, at, h, r = (
+        jnp.arange(n, dtype=jnp.int32).reshape((-1,) + (1,) * (4 - k))
+        for k, n in enumerate((2, short // 8, 2, 8))
+    )
+    ky = (4 * (zone * short + at * 8 + r) + 2 * h + side).astype(jnp.float32)
+    scan_factors = jnp.stack(
+        [jnp.stack(prop_factors(float(CF * n), kx_low, ky, grid_size)) for n in (1, 2)]
+    )
+    held = (landed, factors, scan_factors, tables, first, second)
+    landed, factors, scan_factors, tables, first, second = lax.optimization_barrier(held)
+    off, sums = fine_steps(landed, factors, scan_factors, tables, grid_size, kept, low, slabs, where)
+    return tuple(finish(first, second, sums, off, zone, low))
 
 
 def solution(mesh):

time: 305 us -> 251 us (0.82)
  the two profiles are of different devices: /device:TPU:0 before, /device:TPU:14 now
where the time goes in v1:
time: 251 us; the launch traced here: 250 us
  Pallas kernels  174 us (69%)
  other arithmetic  43.2 us (17%)
  starting transfers between devices  19.8 us (8%)
  waiting for transfers between devices  9.67 us (4%)
    pallas_call x1, Pallas kernels, fine_steps(): pl.pallas_call(kernel, in_specs=[pl.BlockSpec(memory_space=pl.ANY)] * gro...  159 us
    ppermute x4, starting transfers between devices, shards(): landed.append(lax.ppermute(piece, EVERY, links))  17.9 us
    ppermute x4, waiting for transfers between devices, shards(): landed.append(lax.ppermute(piece, EVERY, links))  9.66 us
    pallas_call x1, Pallas kernels, finish(): pl.pallas_call(kernel, grid=(3, 2), in_specs=[whole_smem(), whole, whole,...  7.87 us
    div x2, other arithmetic, prop_factors(): first_coef = jnp.sin(phase_angle) / frequency  7.6 us
    pallas_call x1, Pallas kernels, deal(): pl.pallas_call(kernel, grid=(3, 2), in_specs=[whole_smem(), pl.BlockSpec(...  7.11 us
    mul x2, other arithmetic, apply_parts(): (x + first * m1 + second * n1) * damp  6.98 us
    mul x1, other arithmetic, apply_parts(): (y + first * m2 + second * n2) * damp  5.56 us
  transfers between devices with their start and end apart: 5, of which 1 were waited for; matrix products, arithmetic and copies ran while one was open for 17% of the time, Pallas kernels for 3%

profile of v1, /device:TPU:14, one launch (start us, length us, event | category | flops | bytes accessed | tf_op | source)
XLA Modules:
  0.0 249.6 jit_solution(9199700337442847254)
XLA Ops:
  0.6 1.9 collective-permute-start.4
  2.6 0.6 pad_add_fusion.at_ref
  3.2 7.1 %deal.1 = (f32[2,3,2,32,1024]{4,3,2,1,0:T(8,128)}, f32[2,3,2,32,1024]{4,3,2,1,0:T(8,128)}, f32[2,3,2,32,1024]{4,3,2,1,0:T(8,128)}, f32[2,3,2,32,1024]{4,3,2,1,0:T(8,128)}) custom-call(s32[2]{0:T(128)} %pad_add_fusion.at_ref, f32[1,3,2,128,1024]{4,3,2,1,0:T(8,128)} %c_ref.1, f32[3,2,128,1024]{3,2,1,0:T(8,128)} %i_ref.1), custom_call_target="tpu_custom_call" | custom-call | tf_op jit(solution)/shard_map/deal/pallas_call | solution.py:187
  10.3 1.3 collective-permute-start
  11.6 13.4 %collective-permute-start.1 = (f32[2,3,2,32,1024]{4,3,2,1,0:T(8,128)}, f32[2,3,2,32,1024]{4,3,2,1,0:T(8,128)}, u32[]{:S(2)}, u32[]{:S(2)}) collective-permute-start(f32[2,3,2,32,1024]{4,3,2,1,0:T(8,128)} %get-tuple-element.25), channel_id=1, source_target_pairs={{1,1},{3,5},{5,2},{7,6},{9,9},{11,13},{13,10},{15,14},{17,17},{19,... | collective-permute-start | bytes 4718600 | tf_op jit(solution)/shard_map/ppermute | solution.py:731
  24.9 1.3 collective-permute-start.2
  26.2 1.9 collective-permute-start.3
  28.3 1.5 cosine_multiply_fusion.1
  29.8 0.8 fusion.94
  30.6 3.2 %cosine_multiply_fusion = (f32[4,256,128]{2,1,0:T(8,128)}, f32[4,256,128]{2,1,0:T(8,128)}) fusion(f32[4,128]{1,0:T(4,128)S(1)} %select_multiply_fusion, s32[4,128]{1,0:T(4,128)S(1)} %iota_add_fusion), kind=kLoop, calls=%fused_computation.134 | loop fusion | flops 2097152 | bytes 1052672 | tf_op jit(solution)/shard_map/mul | solution.py:130
  33.9 0.0 copy-start.2
  33.9 0.0 copy-start.3
  33.9 1.0 maximum_bitcast_fusion.13
  34.9 0.9 maximum_bitcast_fusion.12
  35.9 0.1 reduce-precision_convert_fusion.3
  36.0 0.8 pad_maximum_fusion.10.refs_8_
  36.8 1.0 maximum_bitcast_fusion.14
  37.8 0.1 reduce-precision_convert_fusion.1
  37.9 0.9 pad_maximum_fusion.6.refs_9_
  38.9 0.0 copy-done.2
  38.9 0.0 copy-done.3
  38.9 0.1 slice_bitcast_fusion.5
  39.0 0.1 reduce-precision_convert_fusion.2
  39.1 0.9 pad_maximum_fusion.8.refs_6_
  40.0 0.1 maximum_bitcast_fusion.8
  40.1 0.2 reduce-precision_convert_fusion
  40.2 1.1 pad_maximum_fusion.4.refs_7_
  41.3 0.1 add_multiply_fusion.3
  41.4 0.1 broadcast_add_fusion
  41.5 3.2 %fusion.69 = (f32[1,2,4,2,8,768]{5,4,3,2,1,0:T(8,128)S(1)}, f32[1,2,4,2,8,768]{5,4,3,2,1,0:T(8,128)S(1)}, f32[1,2,4,2,8,768]{5,4,3,2,1,0:T(8,128)S(1)}, f32[1,2,...) fusion(f32[2,4,2,8]{3,2,1,0:T(2,128)S(1)} %convert_multiply_fusion, ...), kind=kLoop, calls=%fused_computation.144 | loop fusion | flops 1671168 | bytes 2362880 | tf_op jit(solution)/shard_map/div | solution.py:79
  44.6 0.2 maximum_bitcast_fusion
  44.8 1.6 pad_maximum_fusion.2.refs_5_
  46.4 0.1 convert_multiply_fusion.1
  46.4 4.4 %fusion.2 = (f32[1,2,128,1024]{3,2,1,0:T(8,128)S(1)}, f32[1,2,128,1024]{3,2,1,0:T(8,128)S(1)}, f32[1,2,128,1024]{3,2,1,0:T(8,128)S(1)}) fusion(f32[2,128]{1,0:T(2,128)S(1)} %convert_multiply_fusion.1, f32[1024]{0:T(1024)S(1)} %fusion.99), kind=kLoop, calls=%fused_computation.14 | loop fusion | flops 2883584 | bytes 3150848 | tf_op jit(solution)/shard_map/div | solution.py:79
  50.9 0.0 copy-start
  50.9 1.9 pad_maximum_fusion.refs_4_
  52.8 1.1 copy-done
  53.9 3.4 %fusion.36 = (f32[1,128,1024]{2,1,0:T(8,128)S(1)}, f32[1,128,1024]{2,1,0:T(8,128)S(1)}, f32[1,128,1024]{2,1,0:T(8,128)S(1)}, f32[1,128,1024]{2,1,0:T(8,128)S(1)}) fusion(f32[3,2,128,1024]{3,2,1,0:T(8,128)S(1)} %copy-done, f32[]{:T(128)S(6)} %convert_element_type.148, f32[1024]{0:T(1024)S(1)} %fusion.97, f32[128]{0:T(128)S(1)} %fusion.100, ...), kind=kLoop, calls=%fused_computation.74 | loop fusion | flops 7864320 | bytes 5252104 | tf_op jit(solution)/shard_map/mul | solution.py:98
  57.3 0.0 collective-permute-done.4
  57.3 0.7 broadcast_select_fusion
  58.0 5.6 %fusion.34 = (f32[1,128,1024]{2,1,0:T(8,128)S(1)}, f32[1,128,1024]{2,1,0:T(8,128)S(1)}, f32[1,128,1024]{2,1,0:T(8,128)S(1)}) fusion(f32[3,2,128,1024]{3,2,1,0:T(8,128)S(1)} %copy-done, f32[]{:T(128)S(6)} %convert_element_type.148, f32[128]{0:T(128)S(1)} %add_convert_fusion, f32[128]{0:T(128)S(1)} %fusion.100, f32[1024]{0:T(1024)S(1)} %fusion.99, ...), kind=kLoop, calls=%fused_computation.72 | loop fusion | flops 8781824 | bytes 6300680 | tf_op jit(solution)/shard_map/mul | solution.py:99
  63.6 0.2 maximum_bitcast_fusion.2
  63.7 3.6 %fusion.44 = (f32[1,128,1024]{2,1,0:T(8,128)S(1)}, f32[1,128,1024]{2,1,0:T(8,128)S(1)}, f32[1,128,1024]{2,1,0:T(8,128)S(1)}, f32[1,128,1024]{2,1,0:T(8,128)S(1)}, f32[1,128,1024]{2,1,0:T(8,128)S(1)}) fusion(f32[3,2,128,1024]{3,2,1,0:T(8,128)S(1)} %broadcast_select_fusion, f32[1024]{0:T(1024)S(1)} %fusion.97, f32[128]{0:T(128)S(1)} %fusion.100, ...), kind=kLoop, calls=%fused_computation.82 | loop fusion | flops 8912896 | bytes 5776384 | tf_op jit(solution)/shard_map/mul | solution.py:98
  67.3 0.2 maximum_bitcast_fusion.5
  67.5 0.2 maximum_bitcast_fusion.4
  67.7 0.0 copy-start.1
  67.7 1.9 pad_maximum_fusion.1.first_ref
  69.5 1.2 copy-done.1
  70.7 2.6 %maximum_subtract_fusion.second_ref = f32[3,2,128,1024]{3,2,1,0:T(8,128)} fusion(f32[1,2,128,1024]{3,2,1,0:T(8,128)S(1)} %get-tuple-element.122, f32[1,2,128,1024]{3,2,1,0:T(8,128)S(1)} %get-tuple-element.120, f32[1,2,128,1024]{3,2,1,0:T(8,128)S(1)} %get-tuple-element.121, f32[1,3,2,128,1024]{4,3,2,1,0:T(8,128)S(1)} %copy-done.1), kind=kLoop, calls=%fused_computation.2 | loop fusion | flops 2359296 | bytes 9437184 | tf_op jit(solution)/shard_map/sub | solution.py:747
  73.3 0.0 collective-permute-done.refs_0_
  73.3 0.0 collective-permute-done.1.refs_1_
  73.3 9.7 %collective-permute-done.2.refs_2_ = f32[2,3,2,32,1024]{4,3,2,1,0:T(8,128)} collective-permute-done((f32[2,3,2,32,1024]{4,3,2,1,0:T(8,128)}, f32[2,3,2,32,1024]{4,3,2,1,0:T(8,128)}, u32[]{:S(2)}, u32[]{:S(2)}) %collective-permute-start.2) | collective-permute-done | bytes 1572896 | tf_op jit(solution)/shard_map/ppermute | solution.py:731
  83.0 0.0 collective-permute-done.3.refs_3_
  83.0 158.7 %fine_steps.1 = (f32[2,4,2,3,2,8,768]{6,5,4,3,2,1,0:T(8,128)}, f32[2,4,2,3,2,8,768]{6,5,4,3,2,1,0:T(8,128)}) custom-call(f32[2,3,2,32,1024]{4,3,2,1,0:T(8,128)} %collective-permute-done.refs_0_, f32[2,3,2,32,1024]{4,3,2,1,0:T(8,128)} %collective-permute-done.1.refs_1_, f32[2,3,2,32,1024]{4,3,2,1,0:T(8,128)} %collective-permute-done.2.refs_2_, ...), custom_call_target="tpu_custom_call" | custom-call | tf_op jit(solution)/shard_map/fine_steps/pallas_call | solution.py:642
  241.7 7.9 %finish.1 = (f32[1,3,2,128,1024]{4,3,2,1,0:T(8,128)}, f32[1,3,2,128,1024]{4,3,2,1,0:T(8,128)}) custom-call(s32[1]{0:T(128)} %bitcast.at_ref, f32[3,2,128,1024]{3,2,1,0:T(8,128)} %pad_maximum_fusion.1.first_ref, f32[3,2,128,1024]{3,2,1,0:T(8,128)} %maximum_subtract_fusion.second_ref, f32[2,4,2,3,2,8,768]{6,5,4,3,2,1,0:T(8,128)} %get-tuple-element.44.sum_ref, ...), custom_call_target="tpu_custom_call" | custom-call | tf_op jit(solution)/shard_map/finish/pallas_call | solution.py:696
  (18 shorter events, 0.2 us)
Async XLA Ops:
  0.6 56.7 %collective-permute-start.4 = (f32[3,2,128,1024]{3,2,1,0:T(8,128)}, f32[3,2,128,1024]{3,2,1,0:T(8,128)S(1)}, u32[]{:S(2)}, u32[]{:S(2)}) collective-permute-start(f32[3,2,128,1024]{3,2,1,0:T(8,128)} %bitcast.341), channel_id=1, source_target_pairs={{0,4},{1,5},{2,6},{3,7},{4,8},{5,9},{6,10},{7,11},{8,12},{9,13},{1... | collective-permute-start | bytes 9437192 | tf_op jit(solution)/shard_map/ppermute | solution.py:733
  10.3 63.1 %collective-permute-start = (f32[2,3,2,32,1024]{4,3,2,1,0:T(8,128)}, f32[2,3,2,32,1024]{4,3,2,1,0:T(8,128)}, u32[]{:S(2)}, u32[]{:S(2)}) collective-permute-start(f32[2,3,2,32,1024]{4,3,2,1,0:T(8,128)} %get-tuple-element.24), channel_id=1, source_target_pairs={{0,1},{2,5},{4,2},{6,6},{8,9},{10,13},{12,10},{14,14},{16,17},{18,... | collective-permute-start | bytes 4718600 | tf_op jit(solution)/shard_map/ppermute | solution.py:731
  11.6 61.8 %collective-permute-start.1 = (f32[2,3,2,32,1024]{4,3,2,1,0:T(8,128)}, f32[2,3,2,32,1024]{4,3,2,1,0:T(8,128)}, u32[]{:S(2)}, u32[]{:S(2)}) collective-permute-start(f32[2,3,2,32,1024]{4,3,2,1,0:T(8,128)} %get-tuple-element.25), channel_id=1, source_target_pairs={{1,1},{3,5},{5,2},{7,6},{9,9},{11,13},{13,10},{15,14},{17,17},{19,... | collective-permute-start | bytes 4718600 | tf_op jit(solution)/shard_map/ppermute | solution.py:731
  24.9 58.1 %collective-permute-start.2 = (f32[2,3,2,32,1024]{4,3,2,1,0:T(8,128)}, f32[2,3,2,32,1024]{4,3,2,1,0:T(8,128)}, u32[]{:S(2)}, u32[]{:S(2)}) collective-permute-start(f32[2,3,2,32,1024]{4,3,2,1,0:T(8,128)} %get-tuple-element.26), channel_id=1, source_target_pairs={{2,1},{0,5},{6,2},{4,6},{10,9},{8,13},{14,10},{12,14},{18,17},{16,... | collective-permute-start | bytes 4718600 | tf_op jit(solution)/shard_map/ppermute | solution.py:731
  26.2 56.8 %collective-permute-start.3 = (f32[2,3,2,32,1024]{4,3,2,1,0:T(8,128)}, f32[2,3,2,32,1024]{4,3,2,1,0:T(8,128)}, u32[]{:S(2)}, u32[]{:S(2)}) collective-permute-start(f32[2,3,2,32,1024]{4,3,2,1,0:T(8,128)} %get-tuple-element.27), channel_id=1, source_target_pairs={{3,1},{1,5},{7,2},{5,6},{11,9},{9,13},{15,10},{13,14},{19,17},{17,... | collective-permute-start | bytes 4718600 | tf_op jit(solution)/shard_map/ppermute | solution.py:731
  33.9 5.0 %copy-start.2 = (f32[4,256,128]{2,1,0:T(8,128)S(1)}, f32[4,256,128]{2,1,0:T(8,128)}, u32[]{:S(2)}) copy-start(f32[4,256,128]{2,1,0:T(8,128)} %get-tuple-element.99) | copy-start | bytes 1572868
  33.9 5.0 %copy-start.3 = (f32[4,256,128]{2,1,0:T(8,128)S(1)}, f32[4,256,128]{2,1,0:T(8,128)}, u32[]{:S(2)}) copy-start(f32[4,256,128]{2,1,0:T(8,128)} %get-tuple-element.100) | copy-start | bytes 1572868
  50.9 3.0 %copy-start = (f32[3,2,128,1024]{3,2,1,0:T(8,128)S(1)}, f32[3,2,128,1024]{3,2,1,0:T(8,128)}, u32[]{:S(2)}) copy-start(f32[3,2,128,1024]{3,2,1,0:T(8,128)} %i_ref.1) | copy-start | bytes 9437188
  67.7 3.0 %copy-start.1 = (f32[1,3,2,128,1024]{4,3,2,1,0:T(8,128)S(1)}, f32[1,3,2,128,1024]{4,3,2,1,0:T(8,128)}, u32[]{:S(2)}) copy-start(f32[1,3,2,128,1024]{4,3,2,1,0:T(8,128)} %c_ref.1) | copy-start | bytes 9437188

commit v2 on v1

--- a/solution.py
+++ b/solution.py
@@ -63,10 +63,12 @@
     n = np.arange(lanes)
     angle = 2.0 * np.pi * (n[:, None] * n[None, :] % lanes) / lanes
     c, s = np.cos(angle), sign * np.sin(angle)
-    full = jnp.asarray(np.block([[c, s], [-s, c]]), jnp.float32)
+    full = np.block([[c, s], [-s, c]]).astype(np.float32)
+    high = full.astype(jnp.bfloat16)
+    low = (full - high.astype(np.float32)).astype(jnp.bfloat16)
     turn = 2.0 * np.pi * (np.arange(RADIX)[:, None] * n[None, :]) / grid_size
     twiddle = np.stack([np.cos(turn), sign * np.sin(turn)]).astype(np.float32)
-    return table_pair(full), jnp.asarray(twiddle)
+    return jnp.asarray(np.stack([high, low])), jnp.asarray(twiddle)
 
 
 def prop_factors(steps, wave_x, wave_y, grid_size):
@@ -104,195 +106,270 @@
     return ((real[0], imag[0]), (real[1], imag[1]), (imag[2], -real[2]))
 
 
-def apply_array(state, factors, kx, ky):
-    fields = tuple((state[f, 0], state[f, 1]) for f in range(3))
-    made = apply_parts(fields, factors, kx, ky)
-    return jnp.stack([jnp.stack(pair) for pair in made])
-
-
-def waves_x(grid_size):
-    counter = jnp.arange(grid_size, dtype=jnp.int32)
-    return jnp.where(counter < grid_size // 2, counter, counter - grid_size).astype(jnp.float32)[None]
-
-
-def row_tables(grid_size, kept):
-    quarter, per = grid_size // 4, grid_size // 8
-    y = jnp.arange(quarter, dtype=jnp.int32)
-    q = jnp.arange(4, dtype=jnp.int32)
-    ky = 4 * jnp.arange(per, dtype=jnp.int32)[None] + q[:, None]
-
-    def waves(turns):
-        angle = 2.0 * math.pi / grid_size * (turns % grid_size).astype(jnp.float32)
-        return jnp.cos(angle) / grid_size, jnp.sin(angle) / grid_size
-
-    c, s = waves(y[None, :, None] * ky[:, None, :])
-    weight = jnp.where(ky == 0, 1.0, 2.0).astype(jnp.float32)[:, None, :]
-    c, s = c * weight, s * weight
-    inv_even = jnp.stack([jnp.concatenate([c[k], -s[k]], axis=1) for k in (0, 2)])
-    inv_odd = jnp.concatenate(
-        [
-            jnp.concatenate([c[1], -s[1], c[3], -s[3]], axis=1),
-            jnp.concatenate([s[1], c[1], -s[3], -c[3]], axis=1),
-        ],
-        axis=0,
-    )
-    c, s = waves(ky[:, :kept, None] * y[None, None, :])
-    fwd_even = jnp.stack([jnp.concatenate([c[k], -s[k]], axis=0) for k in (0, 2)])
-    fwd_odd = jnp.concatenate(
-        [
-            jnp.concatenate([c[1], -s[1]], axis=1),
-            jnp.concatenate([-s[1], -c[1]], axis=1),
-            jnp.concatenate([c[3], s[3]], axis=1),
-            jnp.concatenate([-s[3], c[3]], axis=1),
-        ],
-        axis=0,
-    )
-    return [table_pair(t) for t in (inv_even, inv_odd, fwd_even, fwd_odd)]
-
-
-def scalars(*values):
-    return jnp.stack([jnp.asarray(v, jnp.int32) for v in values])
-
-
-def whole_smem():
-    return pl.BlockSpec(memory_space=pltpu.SMEM)
-
-
-def deal(c_state, init, last, ident, group):
-    _, _, _, rows, grid_size = c_state.shape
-    per = rows // 4
-
-    def kernel(at_ref, c_ref, i_ref, *refs):
-        outs, held, dealt = refs[:group], refs[group], refs[group + 1]
-        tile = held.shape[2]
-
-        @pl.when(at_ref[0] > 0)
-        def _():
-            for n in range(held.shape[0]):
-                held[n] = i_ref[0, 0, :, n * tile : (n + 1) * tile]
-
-        @pl.when(at_ref[0] == 0)
-        def _():
-            for n in range(held.shape[0]):
-                held[n] = c_ref[0, 0, 0, :, n * tile : (n + 1) * tile]
-
-        for q in range(4):
-            for n in range(held.shape[0]):
-                dealt[q, :, n * tile : (n + 1) * tile] = held[n, pl.ds(q, per, stride=4), :]
-        for turn in range(group):
-            side = lax.rem(at_ref[1] + group - turn, group) // (group // 2)
-            for h in range(2):
-                outs[turn][h, 0, 0] = dealt[side + 2 * h]
-
-    return pl.pallas_call(
-        kernel,
-        grid=(3, 2),
-        in_specs=[
-            whole_smem(),
-            pl.BlockSpec((1, 1, 1, rows, grid_size), lambda f, c: (0, f, c, 0, 0)),
-            pl.BlockSpec((1, 1, rows, grid_size), lambda f, c: (f, c, 0, 0)),
-        ],
-        out_specs=[pl.BlockSpec((2, 1, 1, per, grid_size), lambda f, c: (0, f, c, 0, 0))] * group,
-        out_shape=[jax.ShapeDtypeStruct((2, 3, 2, per, grid_size), jnp.float32)] * group,
-        scratch_shapes=[
-            pltpu.VMEM((grid_size // 128, rows, 128), jnp.float32),
-            pltpu.VMEM((4, per, grid_size), jnp.float32),
-        ],
-        name="deal",
-    )(scalars(last, ident), c_state, init)
-
-
-def fine_steps(landed, factors, scan_factors, tables, grid_size, kept, low, slabs, where):
-    group = len(landed)
+def fine_steps(c_state, init, slabs, group, where):
     chips = slabs // 2
     MESH = pl.DeviceIdType.MESH
-    _, _, _, short, _ = landed[0].shape
+    rows, grid_size = c_state.shape[3:]
+    short = rows // 4
+    third = grid_size // 3
+    kept = -(-(third // 4 + 1) // 8) * 8
+    low = (third // 128 + 1) * 128
     per = grid_size // 8
+    quarter = grid_size // 4
     lanes = grid_size // RADIX
     half = RADIX // 2
     blocks = per // ROWS
-    limit = float(grid_size // 3)
-    zones = -(-(grid_size // 3 + 1) // (4 * short))
+    limit = float(third)
+    zones = -(-(third + 1) // rows)
     dt = COURANT / grid_size
     total = kept // 8
     each = short // 8
-    inv_even, inv_odd, fwd_even, fwd_odd = tables["rows"]
-    inv_x, inv_tw = tables["inv_x"]
-    fwd_x, fwd_tw = tables["fwd_x"]
+    inv_x, inv_tw = lane_tables(grid_size, 1.0)
+    fwd_x, fwd_tw = lane_tables(grid_size, -1.0)
 
     def kernel(*refs):
-        pieces = refs[:group]
-        fac, sfac, ie, io, fe, fo, ix, itw, fx, ftw, off_out, sum_out = refs[group : group + 12]
-        state, fields, modes, delta, sent, off, mates, carry_in, sums = refs[group + 12 : group + 21]
-        load, fsend, frecv, msend, mrecv, bsend, brecv, psend, precv, csend, crecv, ssend, srecv, osem, usem = refs[
-            group + 21 :
-        ]
+        c_ref, i_ref, ix, itw, fx, ftw, off_out, sum_out, prev, wide_out = refs[:10]
+        state, fields, modes, delta, off, mates, carry_in, sums = refs[10:18]
+        fac, sfac, ie, io, fe, fo, held, dealt = refs[18:26]
+        load, vsend, vrecv, gsend, grecv, wsem = refs[26:32]
+        fsend, frecv, msend, mrecv, bsend, brecv, psend, precv, csend, crecv, ssend, srecv, osem, usem = refs[32:]
         ta, me, z = (lax.axis_index(name) for name in EVERY)
         mate = (ta, 1 - me, z)
+        which = jnp.where(z == where[1], 1, 0)
         is_job = (z == where[0]) | (z == where[1])
         is_home = z < zones
         first = ta == 0
-        passes_on = (me == 1) & (ta < chips - 1) & is_home
-        slab = 2 * ta + jnp.where(z == where[1], 1, 0)
-        target = lax.rem(slab + 1, slabs)
+        shifts = (me == 1) & (ta < chips - 1)
+        passes_on = shifts & is_home
+        own_z = jnp.where(me == 1, where[1], where[0])
         own = 2 * ta + me
-        source = lax.rem(own + slabs - 1, slabs)
-        source_z = jnp.where(lax.rem(source, 2) == 1, where[1], where[0])
-        home_is_own = (target == own) & is_job & is_home
+        home_is_own = is_job & is_home & (which == me)
         kx = lax.broadcasted_iota(jnp.int32, (1, grid_size), 1)
         kx = jnp.where(kx < grid_size // 2, kx, kx - grid_size).astype(jnp.float32)
+        kx_low = jnp.concatenate([kx[:, :low], kx[:, grid_size - low :]], axis=1)
         slots = (2 * me, 2 - me)
 
         barrier = pltpu.get_barrier_semaphore()
         pl.semaphore_signal(barrier, inc=1, device_id=mate, device_id_type=MESH)
         for side in range(2):
-            job = (source // 2, side, source_z)
-            is_self = (source // 2 == ta) & (source_z == z) & (me == side)
-
-            @pl.when(is_home & jnp.logical_not(is_self))
+
+            @pl.when(is_home & jnp.logical_not((z == own_z) & (me == side)))
             def _():
-                pl.semaphore_signal(barrier, inc=1, device_id=job, device_id_type=MESH)
+                pl.semaphore_signal(barrier, inc=1, device_id=(ta, side, own_z), device_id_type=MESH)
+
+        for at in range(group):
+
+            @pl.when(is_job & jnp.logical_not((z == at) & (me == which)))
+            def _():
+                pl.semaphore_signal(barrier, inc=1, device_id=(ta, which, at), device_id_type=MESH)
+
+        @pl.when((me == 0) & (ta > 0))
+        def _():
+            pl.semaphore_signal(barrier, inc=1, device_id=(ta - 1, 1, z), device_id_type=MESH)
 
         @pl.when(is_home & (me == 1) & (ta > 0))
         def _():
-            pl.semaphore_signal(barrier, inc=1, device_id=(ta - 1, me, z), device_id_type=MESH)
-
-        loads = []
-        for n in range(group):
-            at = lax.rem(n + me * (group // 2), group) * short
-            loads.append(
+            pl.semaphore_signal(barrier, inc=1, device_id=(ta - 1, 1, z), device_id_type=MESH)
+
+        expected = (
+            3
+            + jnp.where(shifts, 1, 0)
+            + jnp.where(passes_on, 1, 0)
+            - jnp.where(z == own_z, 1, 0)
+            + jnp.where(is_job, zones, 0)
+            - jnp.where(home_is_own, 1, 0)
+        )
+        pl.semaphore_wait(barrier, expected)
+
+        def prev_copy(n):
+            f, c = n // 2, n % 2
+            return pltpu.make_async_remote_copy(
+                c_ref.at[0, f, c],
+                prev.at[f, c],
+                vsend.at[n],
+                vrecv.at[n],
+                device_id=(jnp.where(me == 1, lax.rem(ta + 1, chips), ta), 1 - me, z),
+                device_id_type=MESH,
+            )
+
+        def state_part(n):
+            return state.at[:, n // 2, n % 2, pl.ds(pl.multiple_of(z * short, 8), short)]
+
+        def gather_copy(n, side):
+            return pltpu.make_async_remote_copy(
+                dealt.at[n, side],
+                state_part(n),
+                gsend.at[n, side],
+                grecv.at[n, z],
+                device_id=(ta, side, own_z),
+                device_id_type=MESH,
+            )
+
+        def gather_wait(n, at):
+            row = pl.ds(at * short, short)
+            part = state.at[:, n // 2, n % 2, row]
+            pltpu.make_async_copy(part, part, grecv.at[n, at]).wait()
+
+        @pl.when((me == 0) | shifts)
+        def _():
+            for n in range(6):
+                prev_copy(n).start()
+
+        tiles = grid_size // 128
+
+        def fetch(ref, n):
+            copies = [
                 pltpu.make_async_copy(
-                    pieces[n], state.at[:, :, :, pl.ds(pl.multiple_of(at, 8), short)], load.at[n]
+                    ref.at[n // 2, n % 2, :, pl.ds(at * 128, 128)], held.at[n % 2, at], load.at[n % 2, at]
                 )
-            )
-            loads[-1].start()
-        for copy in loads:
-            copy.wait()
-        expected = 1 + jnp.where(is_job, zones, 0) - jnp.where(home_is_own, 1, 0) + jnp.where(passes_on, 1, 0)
-        pl.semaphore_wait(barrier, expected)
+                for at in range(tiles)
+            ]
+            for copy in copies:
+                copy.start()
+            for copy in copies:
+                copy.wait()
+
+        def send_part(n):
+            @pl.when(own == 0)
+            def _():
+                fetch(i_ref, n)
+
+            @pl.when(own > 0)
+            def _():
+                pltpu.make_async_copy(prev.at[n // 2, n % 2], prev.at[n // 2, n % 2], vrecv.at[n]).wait()
+                fetch(prev, n)
+
+            for q in range(4):
+                for at in range(tiles):
+                    dealt[n, q % 2, q // 2, :, at * 128 : (at + 1) * 128] = held[
+                        n % 2, at, pl.ds(q, short, stride=4), :
+                    ]
+            for side in range(2):
+                here = (z == own_z) & (me == side)
+
+                @pl.when(here)
+                def _():
+                    pltpu.make_async_copy(dealt.at[n, side], state_part(n), grecv.at[n, z]).start()
+
+                @pl.when(jnp.logical_not(here))
+                def _():
+                    gather_copy(n, side).start()
+
+        def waves(turns):
+            angle = 2.0 * math.pi / grid_size * (turns & (grid_size - 1)).astype(jnp.float32)
+            return jnp.cos(angle) / grid_size, jnp.sin(angle) / grid_size
+
+        def put_pair(ref, lead, row, lane, values):
+            for part, value in enumerate(split_pair(values)):
+                ref[(*lead, part, row, lane)] = value
+
+        def inverse_tables():
+            for q in range(4):
+                for at in range(0, quarter, 64):
+                    y = lax.broadcasted_iota(jnp.int32, (64, per), 0) + at
+                    ky = 4 * lax.broadcasted_iota(jnp.int32, (64, per), 1) + q
+                    c, s = waves(y * ky)
+                    weight = jnp.where(ky == 0, 1.0, 2.0)
+                    c, s = c * weight, s * weight
+                    row, next_row = slice(at, at + 64), slice(quarter + at, quarter + at + 64)
+                    if q % 2 == 0:
+                        put_pair(ie, (q // 2,), row, slice(0, per), c)
+                        put_pair(ie, (q // 2,), row, slice(per, 2 * per), -s)
+                    else:
+                        base = (q // 2) * 2 * per
+                        sign = 1.0 if q == 1 else -1.0
+                        put_pair(io, (), row, slice(base, base + per), c)
+                        put_pair(io, (), row, slice(base + per, base + 2 * per), -s)
+                        put_pair(io, (), next_row, slice(base, base + per), sign * s)
+                        put_pair(io, (), next_row, slice(base + per, base + 2 * per), sign * c)
+
+        def forward_tables():
+            for q in range(4):
+                y = lax.broadcasted_iota(jnp.int32, (kept, quarter), 1)
+                ky = 4 * lax.broadcasted_iota(jnp.int32, (kept, quarter), 0) + q
+                c, s = waves(y * ky)
+                if q % 2 == 0:
+                    both = jnp.concatenate([c, -s], axis=0)
+                    put_pair(fe, (q // 2,), slice(None), slice(None), both)
+                else:
+                    sign = 1.0 if q == 1 else -1.0
+                    both = jnp.concatenate(
+                        [
+                            jnp.concatenate([c, -sign * s], axis=1),
+                            jnp.concatenate([-s, -sign * c], axis=1),
+                        ],
+                        axis=0,
+                    )
+                    base = (q // 2) * 2 * kept
+                    put_pair(fo, (), slice(base, base + 2 * kept), slice(None), both)
+
+        def fine_factors(h):
+            def body(b, carry):
+                at = pl.multiple_of(b * 16, 16)
+                made = prop_factors(1.0, kx, rows_ky(h, at, 16), grid_size)
+                for n in range(3):
+                    fac[n, h, pl.ds(at, 16)] = made[n]
+                return carry
+
+            lax.fori_loop(0, per // 16, body, 0)
+
+        def scan_factors():
+            def body(b, carry):
+                at = b // 4
+                side, h = b // 2 % 2, b % 2
+                m = lax.broadcasted_iota(jnp.int32, (8, 1), 0) + (z * short + at * 8)
+                ky = (4 * m + 2 * h + side).astype(jnp.float32)
+                for k in range(2):
+                    made = prop_factors(float(CF * (k + 1)), kx_low, ky, grid_size)
+                    for n in range(3):
+                        sfac[k, n, side, at, h] = made[n]
+                return carry
+
+            lax.fori_loop(0, 4 * each, body, 0)
+
+        def wide_factors():
+            def body(b, carry):
+                at = pl.multiple_of(b * 8, 8)
+                for part in range(2):
+                    m = lax.broadcasted_iota(jnp.int32, (8, 1), 0) + (z * rows + part * (rows // 2) + at)
+                    ky = m.astype(jnp.float32)
+                    for k, steps in enumerate(((CF * (own + 1)).astype(jnp.float32), float(CF))):
+                        made = prop_factors(steps, kx, ky, grid_size)
+                        for n in range(3):
+                            delta[k, n, part, pl.ds(at, 8)] = made[n]
+                return carry
+
+            lax.fori_loop(0, rows // 16, body, 0)
+            wide_copy().start()
+
+        def wide_copy():
+            return pltpu.make_async_copy(delta.at[:, :, :, : rows // 2], wide_out, wsem)
+
+        def back_part(i):
+            return delta.at[:, :, :, pl.ds(pl.multiple_of(i * 8, 8), 8), : 2 * low]
 
         def back_copy(i):
             return pltpu.make_async_remote_copy(
-                sent.at[i],
+                back_part(i),
                 off.at[me, lax.rem(i, each)],
                 bsend.at[i],
                 brecv.at[me, lax.rem(i, each)],
-                device_id=(target // 2, lax.rem(target, 2), i // each),
+                device_id=(ta, which, i // each),
                 device_id_type=MESH,
             )
 
         def stays(i):
             return home_is_own & (i // each == z)
 
-        def field_copy(b):
-            h, at = b // blocks, pl.multiple_of(b % blocks * ROWS, ROWS)
+        def field_copy(f, h):
+            lane = slice(f * lanes, (f + 1) * lanes)
             return pltpu.make_async_remote_copy(
-                fields.at[2, :, h, :, pl.ds(at, ROWS)],
-                fields.at[me, :, h, :, pl.ds(at, ROWS)],
-                fsend.at[b],
-                frecv.at[b],
+                fields.at[2, :, h, :, :, lane],
+                fields.at[me, :, h, :, :, lane],
+                fsend.at[f, h],
+                frecv.at[f, h],
                 device_id=mate,
-                device_id_type=pl.DeviceIdType.MESH,
+                device_id_type=MESH,
             )
 
         def mode_copy(j):
@@ -309,14 +386,14 @@
             m = lax.broadcasted_iota(jnp.int32, (count, 1), 0) + at
             return (4 * m + 2 * h + me).astype(jnp.float32)
 
-        def inverse(b, carry):
-            h, at = b // blocks, pl.multiple_of(b % blocks * ROWS, ROWS)
-            ky = rows_ky(h, at, ROWS)
-            row = pl.ds(at, ROWS)
-            for f in range(4):
+        def inverse(f, h):
+            def body(b, carry):
+                at = pl.multiple_of(b * ROWS, ROWS)
+                row = pl.ds(at, ROWS)
                 if f < 3:
                     re, im = state[h, f, 0, row], state[h, f, 1, row]
                 else:
+                    ky = rows_ky(h, at, ROWS)
                     re = ky * state[h, 0, 1, row] - kx * state[h, 1, 1, row]
                     im = kx * state[h, 1, 0, row] - ky * state[h, 0, 0, row]
                 parts = [
@@ -335,8 +412,9 @@
                         fields[slots[k // half], k % half, h, c, row, f * lanes : (f + 1) * lanes] = made[
                             k * ROWS : (k + 1) * ROWS, c * lanes : (c + 1) * lanes
                         ]
-            field_copy(b).start()
-            return carry
+                return carry
+
+            return body
 
         def middle(j, carry):
             def rows(c, h):
@@ -396,8 +474,17 @@
             write(state, at, apply_parts(read(state, at), factors, kx, ky))
             return carry
 
+        def turn_of(n):
+            last = total - (zones - 1) * each
+            m = n - last * zones
+            others = max(zones - 1, 1)
+            early = lax.rem(n, zones) * each + n // zones
+            late = lax.rem(m + others, others) * each + last + m // others
+            return jnp.where(m < 0, early, late)
+
         def forward(step):
-            def body(i, carry):
+            def body(n, carry):
+                i = n if step == 0 else turn_of(n)
                 at, ky, factors = rows_of(i)
 
                 def piece(f, c, k):
@@ -460,13 +547,13 @@
                         for c in range(2):
                             for h in range(2):
                                 value = change[f][c][8 * h : 8 * h + 8]
-                                sent[i, h, f, c, :, :low] = value[:, :low]
-                                sent[i, h, f, c, :, low:] = value[:, grid_size - low :]
+                                delta[h, f, c, pl.ds(at, 8), :low] = value[:, :low]
+                                delta[h, f, c, pl.ds(at, 8), low : 2 * low] = value[:, grid_size - low :]
 
                     @pl.when(stays(i))
                     def _():
-                        at = lax.rem(i, each)
-                        pltpu.make_async_copy(sent.at[i], off.at[me, at], brecv.at[me, at]).start()
+                        to = lax.rem(i, each)
+                        pltpu.make_async_copy(back_part(i), off.at[me, to], brecv.at[me, to]).start()
 
                     @pl.when(is_job & jnp.logical_not(stays(i)))
                     def _():
@@ -476,18 +563,45 @@
 
             return body
 
-        for step in range(CF):
-            lax.fori_loop(0, 2 * blocks, inverse, 0)
-            for b in range(2 * blocks):
-                field_copy(b).wait()
-            lax.fori_loop(0, half, middle, 0)
-            if step < CF - 1:
-                lax.fori_loop(kept // 8, per // 8, plain, 0)
-            for j in range(half):
-                mode_copy(j).wait()
-            lax.fori_loop(0, kept // 8, forward(step), 0)
-
-        kx_low = jnp.concatenate([kx[:, :low], kx[:, grid_size - low :]], axis=1)
+        fillers = (
+            inverse_tables,
+            forward_tables,
+            lambda: fine_factors(0),
+            lambda: fine_factors(1),
+            scan_factors,
+            wide_factors,
+        )
+        for n in range(6):
+            send_part(n)
+            fillers[n]()
+
+        def steps():
+            for step in range(CF):
+                for f in (0, 1, 3, 2):
+                    if step == 0 and f < 3:
+                        for n in (2 * f, 2 * f + 1):
+                            for at in range(group):
+                                gather_wait(n, at)
+                    for h in range(2):
+                        lax.fori_loop(0, blocks, inverse(f, h), 0)
+                        field_copy(f, h).start()
+                if step == 0:
+                    wide_copy().wait()
+                for f in range(4):
+                    for h in range(2):
+                        field_copy(f, h).wait()
+                lax.fori_loop(0, half, middle, 0)
+                if step < CF - 1:
+                    lax.fori_loop(kept // 8, per // 8, plain, 0)
+                for j in range(half):
+                    mode_copy(j).wait()
+                lax.fori_loop(0, kept // 8, forward(step), 0)
+
+        pl.when(is_job)(steps)
+
+        @pl.when(jnp.logical_not(is_job))
+        def _():
+            wide_copy().wait()
 
         def chunk(ref, side, at):
             return tuple(
@@ -627,6 +741,18 @@
 
             over(end)
 
+        @pl.when((me == 0) | shifts)
+        def _():
+            for n in range(6):
+                prev_copy(n).wait_send()
+
+        for n in range(6):
+            for side in range(2):
+
+                @pl.when(jnp.logical_not((z == own_z) & (me == side)))
+                def _():
+                    gather_copy(n, side).wait_send()
+
         @pl.when(is_job)
         def _():
             def end(i, carry):
@@ -638,126 +764,115 @@
 
             lax.fori_loop(0, total, end, 0)
 
-    ops = [factors, scan_factors, inv_even, inv_odd, fwd_even, fwd_odd, inv_x, inv_tw, fwd_x, fwd_tw]
     return pl.pallas_call(
         kernel,
-        in_specs=[pl.BlockSpec(memory_space=pl.ANY)] * group
-        + [pl.BlockSpec(memory_space=pltpu.VMEM)] * len(ops),
-        out_specs=[pl.BlockSpec(memory_space=pl.ANY)] * 2,
-        out_shape=[jax.ShapeDtypeStruct((2, each, 2, 3, 2, 8, 2 * low), jnp.float32)] * 2,
+        in_specs=[pl.BlockSpec(memory_space=pl.ANY)] * 2 + [pl.BlockSpec(memory_space=pltpu.VMEM)] * 4,
+        out_specs=[pl.BlockSpec(memory_space=pl.ANY)] * 4,
+        out_shape=[jax.ShapeDtypeStruct((2, each, 2, 3, 2, 8, 2 * low), jnp.float32)] * 2
+        + [
+            jax.ShapeDtypeStruct((3, 2, rows, grid_size), jnp.float32),
+            jax.ShapeDtypeStruct((2, 3, 2, rows // 2, grid_size), jnp.float32),
+        ],
         scratch_shapes=[
             pltpu.VMEM((2, 3, 2, per, grid_size), jnp.float32),
             pltpu.VMEM((3, half, 2, 2, per, 4 * lanes), jnp.float32),
             pltpu.VMEM((3, half, 2, 2, kept, 5 * lanes), jnp.float32),
             pltpu.VMEM((2, 3, 2, kept, grid_size), jnp.float32),
-            pltpu.VMEM((total, 2, 3, 2, 8, 2 * low), jnp.float32),
             *[pltpu.VMEM((2, each, 2, 3, 2, 8, 2 * low), jnp.float32)] * 4,
-            pltpu.SemaphoreType.DMA((group,)),
-            pltpu.SemaphoreType.DMA((2 * blocks,)),
-            pltpu.SemaphoreType.DMA((2 * blocks,)),
+            pltpu.VMEM((3, 2, per, grid_size), jnp.float32),
+            pltpu.VMEM((2, 3, 2, each, 2, 8, 2 * low), jnp.float32),
+            pltpu.VMEM((2, 2, quarter, quarter), jnp.bfloat16),
+            pltpu.VMEM((2, 2 * quarter, 2 * quarter), jnp.bfloat16),
+            pltpu.VMEM((2, 2, 2 * kept, quarter), jnp.bfloat16),
+            pltpu.VMEM((2, 4 * kept, 2 * quarter), jnp.bfloat16),
+            pltpu.VMEM((2, grid_size // 128, rows, 128), jnp.float32),
+            pltpu.VMEM((6, 2, 2, short, grid_size), jnp.float32),
+            pltpu.SemaphoreType.DMA((2, grid_size // 128)),
+            pltpu.SemaphoreType.DMA((6,)),
+            pltpu.SemaphoreType.DMA((6,)),
+            pltpu.SemaphoreType.DMA((6, 2)),
+            pltpu.SemaphoreType.DMA((6, group)),
+            pltpu.SemaphoreType.DMA,
+            pltpu.SemaphoreType.DMA((4, 2)),
+            pltpu.SemaphoreType.DMA((4, 2)),
             pltpu.SemaphoreType.DMA((half,)),
             pltpu.SemaphoreType.DMA((half,)),
             pltpu.SemaphoreType.DMA((total,)),
             *[pltpu.SemaphoreType.DMA((2, each))] * 9,
         ],
         compiler_params=pltpu.CompilerParams(
-            collective_id=0, has_side_effects=True, vmem_limit_bytes=62 * 1024 * 1024
+            collective_id=0, has_side_effects=True, vmem_limit_bytes=63 * 1024 * 1024
         ),
         name="fine_steps",
-    )(*landed, *ops)
-
-
-def finish(first, second, sums, off, zone, low):
-    _, _, rows, grid_size = first.shape
-    each = sums.shape[1]
-    short = rows // 4
+    )(c_state, init, inv_x, inv_tw, fwd_x, fwd_tw)
+
+
+def scalars(*values):
+    return jnp.stack([jnp.asarray(v, jnp.int32) for v in values])
+
+
+def finish(c_state, init, prev, wide, sums, off, slab, zone):
+    rows, grid_size = c_state.shape[3:]
+    each, low = sums.shape[1], sums.shape[-1] // 2
     limit = grid_size // 3
-
-    def kernel(at_ref, first_ref, second_ref, sum_ref, off_ref, new_ref, res_ref, held):
-        ky = lax.broadcasted_iota(jnp.int32, (rows, 1), 0) + at_ref[0] * rows
-        inside = ky <= limit
-        for base, extra, out in ((first_ref, sum_ref, new_ref), (second_ref, off_ref, res_ref)):
+    step = rows // each
+
+    def kernel(at_ref, c_ref, i_ref, p_ref, w_ref, sum_ref, off_ref, new_ref, res_ref, held):
+        kx = lax.broadcasted_iota(jnp.int32, (1, grid_size), 1)
+        kx = jnp.where(kx < grid_size // 2, kx, kx - grid_size).astype(jnp.float32)
+        row = lax.broadcasted_iota(jnp.int32, (step, 1), 0) + at_ref[1] * rows + pl.program_id(0) * step
+        ky = row.astype(jnp.float32)
+        inside = row <= limit
+
+        def moved(fields, k):
+            return apply_parts(fields, (w_ref[k, 0], w_ref[k, 1], w_ref[k, 2]), kx, ky)
+
+        def placed(ref, f, c):
             for n in range(held.shape[0]):
                 for side in range(2):
                     for h in range(2):
-                        values = extra[side, :, h, 0, 0, :, n * 128 : (n + 1) * 128]
-                        held[n, pl.ds(side + 2 * h, short, stride=4), :] = values.reshape(short, 128)
-            for n in range(held.shape[0]):
-                at = n * 128 if n * 128 < low else grid_size - 2 * low + n * 128
-                lane = slice(at, at + 128)
-                out[0, 0, 0, :, lane] = base[0, 0, :, lane] + jnp.where(inside, held[n], 0.0)
-            if low * 2 < grid_size:
-                lane = slice(low, grid_size - low)
-                out[0, 0, 0, :, lane] = base[0, 0, :, lane]
-
-    whole = pl.BlockSpec((1, 1, rows, grid_size), lambda f, c: (f, c, 0, 0))
-    extra = pl.BlockSpec((2, each, 2, 1, 1, 8, 2 * low), lambda f, c: (0, 0, 0, f, c, 0, 0))
-    out = pl.BlockSpec((1, 1, 1, rows, grid_size), lambda f, c: (0, f, c, 0, 0))
+                        held[n, pl.ds(side + 2 * h, 8, stride=4), :] = ref[
+                            side, 0, h, f, c, :, n * 128 : (n + 1) * 128
+                        ]
+            found = [jnp.where(inside, held[n], 0.0) for n in range(held.shape[0])]
+            count = low // 128
+            between = [jnp.zeros((step, grid_size - 2 * low), jnp.float32)] if 2 * low < grid_size else []
+            return jnp.concatenate(found[:count] + between + found[count:], axis=1)
+
+        is_first = at_ref[0] == 0
+        start = tuple(tuple(i_ref[f, c] for c in range(2)) for f in range(3))
+        before = tuple(tuple(jnp.where(is_first, i_ref[f, c], p_ref[f, c]) for c in range(2)) for f in range(3))
+        new, end = moved(start, 0), moved(before, 1)
+        for f in range(3):
+            for c in range(2):
+                new_ref[0, f, c] = new[f][c] + placed(sum_ref, f, c)
+                res_ref[0, f, c] = (end[f][c] + placed(off_ref, f, c)) - c_ref[0, f, c]
+
+    whole = pl.BlockSpec((1, 3, 2, step, grid_size), lambda i: (0, 0, 0, i, 0))
+    part = pl.BlockSpec((3, 2, step, grid_size), lambda i: (0, 0, i, 0))
+    factor = pl.BlockSpec((2, 3, step, grid_size), lambda i: (0, 0, i, 0))
+    extra = pl.BlockSpec((2, 1, 2, 3, 2, 8, 2 * low), lambda i: (0, i, 0, 0, 0, 0, 0))
     return pl.pallas_call(
         kernel,
-        grid=(3, 2),
-        in_specs=[whole_smem(), whole, whole, extra, extra],
-        out_specs=[out, out],
-        out_shape=[jax.ShapeDtypeStruct((1, *first.shape), jnp.float32)] * 2,
-        scratch_shapes=[pltpu.VMEM((2 * low // 128, rows, 128), jnp.float32)],
+        grid=(each,),
+        in_specs=[pl.BlockSpec(memory_space=pltpu.SMEM), whole, part, part, factor, extra, extra],
+        out_specs=[whole, whole],
+        out_shape=[jax.ShapeDtypeStruct(c_state.shape, jnp.float32)] * 2,
+        scratch_shapes=[pltpu.VMEM((2 * low // 128, step, 128), jnp.float32)],
         name="finish",
-    )(scalars(zone), first, second, sums, off)
+    )(scalars(slab, zone), c_state, init, prev, wide, sums, off)
 
 
 def shards(c_state, init):
     rows, grid_size = c_state.shape[3:]
     group = lax.axis_size(SPACE)
     slabs = lax.axis_size(SLAB)
-    slab = lax.axis_index(SLAB)
-    core = lax.axis_index("core")
-    zone = lax.axis_index(SPACE)
-    short = rows // 4
-    limit = grid_size // 3
-    kept = -(-(limit // 4 + 1) // 8) * 8
-    low = (limit // 128 + 1) * 128
     where = (group // 2 - 1, group // 2)
-
-    def device(k, z):
-        return k * group + z
-
-    pieces = deal(c_state, init, slab == slabs - 1, zone, group)
-    landed = []
-    for n, piece in enumerate(pieces):
-        links = [
-            (device(k, (n + c * (group // 2)) % group), device(k // 2 * 2 + c, where[k % 2]))
-            for k in range(slabs)
-            for c in range(2)
-        ]
-        landed.append(lax.ppermute(piece, EVERY, links))
-    links = [(device(k, z), device(k + 1, z)) for k in range(slabs - 1) for z in range(group)]
-    before = jnp.where(slab == 0, init, lax.ppermute(c_state[0], EVERY, links))
-
-    kx = waves_x(grid_size)
-    tables = {
-        "rows": row_tables(grid_size, kept),
-        "inv_x": lane_tables(grid_size, 1.0),
-        "fwd_x": lane_tables(grid_size, -1.0),
-    }
-    ky = 4 * jnp.arange(grid_size // 8, dtype=jnp.int32)[None] + 2 * jnp.arange(2, dtype=jnp.int32)[:, None]
-    ky = (ky + core).astype(jnp.float32)[:, :, None]
-    factors = jnp.stack(prop_factors(1.0, kx[None], ky, grid_size))
-
-    ky = (zone * rows + jnp.arange(rows, dtype=jnp.int32)).astype(jnp.float32)[:, None]
-    first = apply_array(init, prop_factors((CF * (slab + 1)).astype(jnp.float32), kx, ky, grid_size), kx, ky)
-    second = apply_array(before, prop_factors(float(CF), kx, ky, grid_size), kx, ky) - c_state[0]
-    kx_low = jnp.concatenate([kx[:, :low], kx[:, grid_size - low :]], axis=1)
-    side, at, h, r = (
-        jnp.arange(n, dtype=jnp.int32).reshape((-1,) + (1,) * (4 - k))
-        for k, n in enumerate((2, short // 8, 2, 8))
+    off, sums, prev, wide = fine_steps(c_state, init, slabs, group, where)
+    wide = wide.reshape(2, 3, rows, grid_size)
+    return tuple(
+        finish(c_state, init, prev, wide, sums, off, lax.axis_index(SLAB), lax.axis_index(SPACE))
     )
-    ky = (4 * (zone * short + at * 8 + r) + 2 * h + side).astype(jnp.float32)
-    scan_factors = jnp.stack(
-        [jnp.stack(prop_factors(float(CF * n), kx_low, ky, grid_size)) for n in (1, 2)]
-    )
-    held = (landed, factors, scan_factors, tables, first, second)
-    landed, factors, scan_factors, tables, first, second = lax.optimization_barrier(held)
-    off, sums = fine_steps(landed, factors, scan_factors, tables, grid_size, kept, low, slabs, where)
-    return tuple(finish(first, second, sums, off, zone, low))
 
 
 def solution(mesh):

time: 251 us -> 218 us (0.87)
  other arithmetic: 43.2 us -> 0.6 us
  Pallas kernels: 174 us -> 216 us
  starting transfers between devices: 19.8 us -> 0 us
  waiting for transfers between devices: 9.67 us -> 0 us
    pallas_call x3 -> x2, Pallas kernels: 174 us -> 216 us  [the longest x1 205 us: fine_steps(): pl.pallas_call(kernel, in_specs=[pl.BlockSpec(memory_space=pl.ANY)] * 2 +...]
    ppermute x5 -> x0, starting transfers between devices: 19.8 us -> none  [the longest x4 17.9 us: shards(): landed.append(lax.ppermute(piece, EVERY, links))]
    mul x13 -> x0, other arithmetic: 16 us -> none  [the longest x2 6.98 us: apply_parts(): (x + first * m1 + second * n1) * damp]
    another operation x19 -> x0, other arithmetic: 12.1 us -> none  [the longest x4 3.71 us: table_pair(): return jnp.stack([high, values - high], axis=-3).astype(jnp.bfloat16)]
    ppermute x5 -> x0, waiting for transfers between devices: 9.67 us -> none  [the longest x4 9.66 us: shards(): landed.append(lax.ppermute(piece, EVERY, links))]
    div x3 -> x0, other arithmetic: 9.1 us -> none  [the longest x2 7.6 us: prop_factors(): first_coef = jnp.sin(phase_angle) / frequency]
    sub x1 -> x0, other arithmetic: 2.63 us -> none  [shards(): apply_array(before, prop_factors(float(CF), kx, ky, grid_size), kx, ky)]
  transfers between devices with their start and end apart: 5 -> 0, of which waited for: 1 -> 0; matrix products, arithmetic and copies ran while one was open for 17% -> 0% of each run, Pallas kernels for 3% -> 0%
where the time goes in v2:
time: 218 us
  Pallas kernels  216 us (99%)
    pallas_call x1, Pallas kernels, fine_steps(): pl.pallas_call(kernel, in_specs=[pl.BlockSpec(memory_space=pl.ANY)] * 2 +...  205 us
    pallas_call x1, Pallas kernels, finish(): pl.pallas_call(kernel, grid=(each,), in_specs=[pl.BlockSpec(memory_space=...  10.8 us

profile of v2, /device:TPU:14, one launch (start us, length us, event | category | flops | bytes accessed | tf_op | source)
XLA Modules:
  0.0 217.5 jit_solution(15678029372566325079)
XLA Ops:
  0.6 0.6 pad_add_fusion.at_ref
  1.2 205.4 %fine_steps.1 = (f32[2,4,2,3,2,8,768]{6,5,4,3,2,1,0:T(8,128)}, f32[2,4,2,3,2,8,768]{6,5,4,3,2,1,0:T(8,128)}, f32[3,2,128,1024]{3,2,1,0:T(8,128)}, f32[2,3,2,64,1024]{4,3,2,1,0:T(8,128)}) custom-call(f32[1,3,2,128,1024]{4,3,2,1,0:T(8,128)} %c_ref.1, f32[3,2,128,1024]{3,2,1,0:T(8,128)} %i_ref.1, bf16[2,256,256]{2,1,0:T(8,128)(2,1)} %constant.22.clone.refs_2_, ...), custom_call_target="tpu_custom_call" | custom-call | tf_op jit(solution)/shard_map/fine_steps/pallas_call | solution.py:767
  206.7 10.8 %finish.1 = (f32[1,3,2,128,1024]{4,3,2,1,0:T(8,128)}, f32[1,3,2,128,1024]{4,3,2,1,0:T(8,128)}) custom-call(s32[2]{0:T(128)} %pad_add_fusion.at_ref, f32[1,3,2,128,1024]{4,3,2,1,0:T(8,128)} %c_ref.1, f32[3,2,128,1024]{3,2,1,0:T(8,128)} %i_ref.1, f32[3,2,128,1024]{3,2,1,0:T(8,128)} %get-tuple-element.6.p_ref, f32[2,3,128,1024]{3,2,1,0:T(8,128)} %bitcast.3, ...), custom_call_target="tpu_custom_call" | custom-call | tf_op jit(solution)/shard_map/finish/pallas_call | solution.py:855

commit v3 on v2

--- a/solution.py
+++ b/solution.py
@@ -128,11 +128,11 @@
     fwd_x, fwd_tw = lane_tables(grid_size, -1.0)
 
     def kernel(*refs):
-        c_ref, i_ref, ix, itw, fx, ftw, off_out, sum_out, prev, wide_out = refs[:10]
-        state, fields, modes, delta, off, mates, carry_in, sums = refs[10:18]
-        fac, sfac, ie, io, fe, fo, held, dealt = refs[18:26]
-        load, vsend, vrecv, gsend, grecv, wsem = refs[26:32]
-        fsend, frecv, msend, mrecv, bsend, brecv, psend, precv, csend, crecv, ssend, srecv, osem, usem = refs[32:]
+        c_ref, i_ref, ix, itw, fx, ftw, new_out, res_out, prev = refs[:9]
+        state, fields, modes, delta, off, mates, carry_in, sums = refs[9:17]
+        fac, sfac, ie, io, fe, fo, held, dealt = refs[17:25]
+        load, vsend, vrecv, gsend, grecv, bases = refs[25:31]
+        fsend, frecv, msend, mrecv, bsend, brecv, psend, precv, csend, crecv, ssend, osem = refs[31:]
         ta, me, z = (lax.axis_index(name) for name in EVERY)
         mate = (ta, 1 - me, z)
         which = jnp.where(z == where[1], 1, 0)
@@ -327,33 +327,15 @@
 
             lax.fori_loop(0, 4 * each, body, 0)
 
-        def wide_factors():
-            def body(b, carry):
-                at = pl.multiple_of(b * 8, 8)
-                for part in range(2):
-                    m = lax.broadcasted_iota(jnp.int32, (8, 1), 0) + (z * rows + part * (rows // 2) + at)
-                    ky = m.astype(jnp.float32)
-                    for k, steps in enumerate(((CF * (own + 1)).astype(jnp.float32), float(CF))):
-                        made = prop_factors(steps, kx, ky, grid_size)
-                        for n in range(3):
-                            delta[k, n, part, pl.ds(at, 8)] = made[n]
-                return carry
-
-            lax.fori_loop(0, rows // 16, body, 0)
-            wide_copy().start()
-
-        def wide_copy():
-            return pltpu.make_async_copy(delta.at[:, :, :, : rows // 2], wide_out, wsem)
-
-        def back_part(i):
-            return delta.at[:, :, :, pl.ds(pl.multiple_of(i * 8, 8), 8), : 2 * low]
-
-        def back_copy(i):
+        def back_part(i, h):
+            return delta.at[h, :, :, pl.ds(pl.multiple_of(i * 8, 8), 8), : 2 * low]
+
+        def back_copy(i, h):
             return pltpu.make_async_remote_copy(
-                back_part(i),
-                off.at[me, lax.rem(i, each)],
-                bsend.at[i],
-                brecv.at[me, lax.rem(i, each)],
+                back_part(i, h),
+                off.at[me, lax.rem(i, each), h],
+                bsend.at[i, h],
+                brecv.at[me, lax.rem(i, each), h],
                 device_id=(ta, which, i // each),
                 device_id_type=MESH,
             )
@@ -553,11 +535,15 @@
                     @pl.when(stays(i))
                     def _():
                         to = lax.rem(i, each)
-                        pltpu.make_async_copy(back_part(i), off.at[me, to], brecv.at[me, to]).start()
+                        for h in range(2):
+                            pltpu.make_async_copy(
+                                back_part(i, h), off.at[me, to, h], brecv.at[me, to, h]
+                            ).start()
 
                     @pl.when(is_job & jnp.logical_not(stays(i)))
                     def _():
-                        back_copy(i).start()
+                        for h in range(2):
+                            back_copy(i, h).start()
 
                 return carry
 
@@ -569,11 +555,11 @@
             lambda: fine_factors(0),
             lambda: fine_factors(1),
             scan_factors,
-            wide_factors,
         )
         for n in range(6):
             send_part(n)
-            fillers[n]()
+            if n < len(fillers):
+                fillers[n]()
 
         def steps():
             for step in range(CF):
@@ -583,10 +569,8 @@
                             for at in range(group):
                                 gather_wait(n, at)
                     for h in range(2):
-                        lax.fori_loop(0, blocks, inverse(f, h), 0)
+                        lax.fori_loop(0, blocks, inverse(f, h), 0, unroll=True)
                         field_copy(f, h).start()
-                if step == 0:
-                    wide_copy().wait()
                 for f in range(4):
                     for h in range(2):
                         field_copy(f, h).wait()
@@ -599,147 +583,212 @@
 
         pl.when(is_job)(steps)
 
-        @pl.when(jnp.logical_not(is_job))
+        span = rows // each
+
+        def base_copies():
+            pairs = [(i_ref, state.at[0, :, :, :rows]), (c_ref.at[0], state.at[1, :, :, :rows])]
+            return [pltpu.make_async_copy(ref, to, bases.at[n]) for n, (ref, to) in enumerate(pairs)]
+
+        def before_copy(ref):
+            return pltpu.make_async_copy(ref, fac.at[:, :, :rows], bases.at[2])
+
+        for copy in base_copies():
+            copy.start()
+
+        @pl.when(own == 0)
         def _():
-            wide_copy().wait()
-
-        def chunk(ref, side, at):
-            return tuple(
-                tuple(jnp.concatenate([ref[side, at, h, f, c] for h in range(2)], axis=0) for c in range(2))
-                for f in range(3)
-            )
-
-        def moved(n, values, side, at):
+            before_copy(i_ref).start()
+
+        @pl.when(own > 0)
+        def _():
+            before_copy(prev).start()
+
+        for copy in base_copies():
+            copy.wait()
+        before_copy(prev).wait()
+
+        def base_rows(b, carry):
+            at = pl.multiple_of(b * 8, 8)
+            row = pl.ds(at, 8)
+            m = lax.broadcasted_iota(jnp.int32, (8, 1), 0) + (z * rows + at)
+            ky = m.astype(jnp.float32)
+            for n, steps in enumerate(((CF * (own + 1)).astype(jnp.float32), float(CF))):
+                factors = prop_factors(steps, kx, ky, grid_size)
+                start = tuple(
+                    tuple(state[0, f, c, row] if n == 0 else fac[f, c, row] for c in range(2))
+                    for f in range(3)
+                )
+                made = apply_parts(start, factors, kx, ky)
+                for f in range(3):
+                    for c in range(2):
+                        if n == 0:
+                            state[0, f, c, row] = made[f][c]
+                        else:
+                            state[1, f, c, row] = made[f][c] - state[1, f, c, row]
+            return carry
+
+        lax.fori_loop(0, rows // 8, base_rows, 0)
+
+        def out_copy(n, at):
+            row = pl.ds(pl.multiple_of(at * span, 8), span)
+            to = (new_out, res_out)[n].at[0, :, :, row]
+            return pltpu.make_async_copy(state.at[n, :, :, row], to, osem.at[n, at])
+
+        zone_blocks = jnp.where(is_home, jnp.minimum(each, total - z * each), 0)
+
+        def out_now(at, carry):
+            for n in range(2):
+                out_copy(n, at).start()
+            return carry
+
+        lax.fori_loop(zone_blocks, each, out_now, 0)
+
+        def finish(at):
+            row = pl.ds(pl.multiple_of(at * span, 8), span)
+            for k, ref in enumerate((sums, off)):
+                for f in range(3):
+                    for c in range(2):
+                        for n in range(2 * low // 128):
+                            for side in range(2):
+                                for h in range(2):
+                                    held[c, n, pl.ds(side + 2 * h, 8, stride=4), :] = ref[
+                                        side, at, h, f, c, :, n * 128 : (n + 1) * 128
+                                    ]
+                            lane = n * 128 if n * 128 < low else grid_size - 2 * low + n * 128
+                            lane = slice(lane, lane + 128)
+                            state[k, f, c, row, lane] = state[k, f, c, row, lane] + held[c, n, :span]
+                out_copy(k, at).start()
+
+        def chunk(ref, side, at, h):
+            return tuple(tuple(ref[side, at, h, f, c] for c in range(2)) for f in range(3))
+
+        def moved(n, values, side, at, h):
             m = lax.broadcasted_iota(jnp.int32, (8, 1), 0) + (z * short + at * 8)
-            ky = jnp.concatenate([4 * m + 2 * h + side for h in range(2)], axis=0).astype(jnp.float32)
-            factors = tuple(
-                jnp.concatenate([sfac[n, k, side, at, h] for h in range(2)], axis=0) for k in range(3)
-            )
+            ky = (4 * m + 2 * h + side).astype(jnp.float32)
+            factors = tuple(sfac[n, k, side, at, h] for k in range(3))
             return apply_parts(values, factors, kx_low, ky)
 
-        def put(side, at, values):
+        def put(side, at, h, values):
             for f in range(3):
                 for c in range(2):
-                    for h in range(2):
-                        sums[side, at, h, f, c] = values[f][c][8 * h : 8 * h + 8]
-            pltpu.make_async_copy(sums.at[side, at], sum_out.at[side, at], usem.at[side, at]).start()
+                    sums[side, at, h, f, c] = values[f][c]
 
         def plus(left, right):
             return tuple(tuple(a + b for a, b in zip(p, q)) for p, q in zip(left, right))
 
-        def landed_copy(side, at):
-            return pltpu.make_async_copy(off.at[side, at], off.at[side, at], brecv.at[side, at])
-
-        def off_copy(side, at):
-            return pltpu.make_async_copy(off.at[side, at], off_out.at[side, at], osem.at[side, at])
-
-        def pair_copy(side, at):
+        def landed_copy(side, at, h):
+            part = off.at[side, at, h]
+            return pltpu.make_async_copy(part, part, brecv.at[side, at, h])
+
+        def pair_copy(side, at, h):
             return pltpu.make_async_remote_copy(
-                off.at[side, at],
-                mates.at[side, at],
-                psend.at[side, at],
-                precv.at[side, at],
+                off.at[side, at, h],
+                mates.at[side, at, h],
+                psend.at[side, at, h],
+                precv.at[side, at, h],
                 device_id=(ta, 1, z),
                 device_id_type=MESH,
             )
 
-        def share_copy(side, at):
+        def share_copy(side, at, h):
             return pltpu.make_async_remote_copy(
-                carry_in.at[side, at],
-                carry_in.at[side, at],
-                csend.at[side, at],
-                crecv.at[side, at],
+                carry_in.at[side, at, h],
+                carry_in.at[side, at, h],
+                csend.at[side, at, h],
+                crecv.at[side, at, h],
                 device_id=(ta, 0, z),
                 device_id_type=MESH,
             )
 
-        def chain_copy(side, at):
+        def chain_copy(side, at, h):
             return pltpu.make_async_remote_copy(
-                sums.at[side, at],
-                carry_in.at[side, at],
-                ssend.at[side, at],
-                crecv.at[side, at],
+                sums.at[side, at, h],
+                carry_in.at[side, at, h],
+                ssend.at[side, at, h],
+                crecv.at[side, at, h],
                 device_id=(lax.rem(ta + 1, chips), 1, z),
                 device_id_type=MESH,
             )
 
-        mine = jnp.minimum(each, total - z * each) * 2
-
         def over(body):
             def step(t, carry):
-                body(lax.rem(t, 2), t // 2)
+                body(lax.rem(t, 2), t // 4, lax.rem(t // 2, 2))
                 return carry
 
-            lax.fori_loop(0, mine, step, 0)
+            lax.fori_loop(0, zone_blocks * 4, step, 0)
+
+        def end_group(side, at, h):
+            @pl.when(side + h == 2)
+            def _():
+                finish(at)
 
         @pl.when(is_home & (me == 0))
         def _():
-            def start(side, at):
-                landed_copy(side, at).wait()
-                pair_copy(side, at).start()
-                off_copy(side, at).start()
+            def start(side, at, h):
+                landed_copy(side, at, h).wait()
+                pair_copy(side, at, h).start()
 
             over(start)
 
-            def rest(side, at):
+            def rest(side, at, h):
                 @pl.when(first)
                 def _():
-                    put(side, at, chunk(off, side, at))
+                    put(side, at, h, chunk(off, side, at, h))
 
                 @pl.when(ta > 0)
                 def _():
-                    share_copy(side, at).wait_recv()
-                    put(side, at, plus(chunk(off, side, at), moved(0, chunk(carry_in, side, at), side, at)))
+                    share_copy(side, at, h).wait_recv()
+                    carried = moved(0, chunk(carry_in, side, at, h), side, at, h)
+                    put(side, at, h, plus(chunk(off, side, at, h), carried))
+
+                end_group(side, at, h)
 
             over(rest)
 
-            def end(side, at):
-                pair_copy(side, at).wait_send()
+            def end(side, at, h):
+                pair_copy(side, at, h).wait_send()
 
             over(end)
 
         @pl.when(is_home & (me == 1))
         def _():
-            def step(side, at):
-                landed_copy(side, at).wait()
-                off_copy(side, at).start()
-                pair_copy(side, at).wait_recv()
-                both = plus(chunk(off, side, at), moved(0, chunk(mates, side, at), side, at))
+            def step(side, at, h):
+                landed_copy(side, at, h).wait()
+                pair_copy(side, at, h).wait_recv()
+                both = plus(chunk(off, side, at, h), moved(0, chunk(mates, side, at, h), side, at, h))
 
                 @pl.when(first)
                 def _():
-                    put(side, at, both)
+                    put(side, at, h, both)
 
                 @pl.when(ta > 0)
                 def _():
-                    chain_copy(side, at).wait_recv()
-                    share_copy(side, at).start()
-                    put(side, at, plus(both, moved(1, chunk(carry_in, side, at), side, at)))
+                    chain_copy(side, at, h).wait_recv()
+                    share_copy(side, at, h).start()
+                    put(side, at, h, plus(both, moved(1, chunk(carry_in, side, at, h), side, at, h)))
 
                 @pl.when(passes_on)
                 def _():
-                    chain_copy(side, at).start()
+                    chain_copy(side, at, h).start()
+
+                end_group(side, at, h)
 
             over(step)
 
-            def end(side, at):
+            def end(side, at, h):
                 @pl.when(ta > 0)
                 def _():
-                    share_copy(side, at).wait_send()
+                    share_copy(side, at, h).wait_send()
 
                 @pl.when(passes_on)
                 def _():
-                    chain_copy(side, at).wait_send()
+                    chain_copy(side, at, h).wait_send()
 
             over(end)
 
-        @pl.when(is_home)
-        def _():
-            def end(side, at):
-                off_copy(side, at).wait()
-                pltpu.make_async_copy(sums.at[side, at], sum_out.at[side, at], usem.at[side, at]).wait()
-
-            over(end)
+        for n in range(2):
+            for at in range(each):
+                out_copy(n, at).wait()
 
         @pl.when((me == 0) | shifts)
         def _():
@@ -758,7 +807,8 @@
             def end(i, carry):
                 @pl.when(jnp.logical_not(stays(i)))
                 def _():
-                    back_copy(i).wait_send()
+                    for h in range(2):
+                        back_copy(i, h).wait_send()
 
                 return carry
 
@@ -767,12 +817,9 @@
     return pl.pallas_call(
         kernel,
         in_specs=[pl.BlockSpec(memory_space=pl.ANY)] * 2 + [pl.BlockSpec(memory_space=pltpu.VMEM)] * 4,
-        out_specs=[pl.BlockSpec(memory_space=pl.ANY)] * 4,
-        out_shape=[jax.ShapeDtypeStruct((2, each, 2, 3, 2, 8, 2 * low), jnp.float32)] * 2
-        + [
-            jax.ShapeDtypeStruct((3, 2, rows, grid_size), jnp.float32),
-            jax.ShapeDtypeStruct((2, 3, 2, rows // 2, grid_size), jnp.float32),
-        ],
+        out_specs=[pl.BlockSpec(memory_space=pl.ANY)] * 3,
+        out_shape=[jax.ShapeDtypeStruct(c_state.shape, jnp.float32)] * 2
+        + [jax.ShapeDtypeStruct((3, 2, rows, grid_size), jnp.float32)],
         scratch_shapes=[
             pltpu.VMEM((2, 3, 2, per, grid_size), jnp.float32),
             pltpu.VMEM((3, half, 2, 2, per, 4 * lanes), jnp.float32),
@@ -792,13 +839,14 @@
             pltpu.SemaphoreType.DMA((6,)),
             pltpu.SemaphoreType.DMA((6, 2)),
             pltpu.SemaphoreType.DMA((6, group)),
-            pltpu.SemaphoreType.DMA,
+            pltpu.SemaphoreType.DMA((3,)),
             pltpu.SemaphoreType.DMA((4, 2)),
             pltpu.SemaphoreType.DMA((4, 2)),
             pltpu.SemaphoreType.DMA((half,)),
             pltpu.SemaphoreType.DMA((half,)),
-            pltpu.SemaphoreType.DMA((total,)),
-            *[pltpu.SemaphoreType.DMA((2, each))] * 9,
+            pltpu.SemaphoreType.DMA((total, 2)),
+            *[pltpu.SemaphoreType.DMA((2, each, 2))] * 6,
+            pltpu.SemaphoreType.DMA((2, each)),
         ],
         compiler_params=pltpu.CompilerParams(
             collective_id=0, has_side_effects=True, vmem_limit_bytes=63 * 1024 * 1024
@@ -807,72 +855,11 @@
     )(c_state, init, inv_x, inv_tw, fwd_x, fwd_tw)
 
 
-def scalars(*values):
-    return jnp.stack([jnp.asarray(v, jnp.int32) for v in values])
-
-
-def finish(c_state, init, prev, wide, sums, off, slab, zone):
-    rows, grid_size = c_state.shape[3:]
-    each, low = sums.shape[1], sums.shape[-1] // 2
-    limit = grid_size // 3
-    step = rows // each
-
-    def kernel(at_ref, c_ref, i_ref, p_ref, w_ref, sum_ref, off_ref, new_ref, res_ref, held):
-        kx = lax.broadcasted_iota(jnp.int32, (1, grid_size), 1)
-        kx = jnp.where(kx < grid_size // 2, kx, kx - grid_size).astype(jnp.float32)
-        row = lax.broadcasted_iota(jnp.int32, (step, 1), 0) + at_ref[1] * rows + pl.program_id(0) * step
-        ky = row.astype(jnp.float32)
-        inside = row <= limit
-
-        def moved(fields, k):
-            return apply_parts(fields, (w_ref[k, 0], w_ref[k, 1], w_ref[k, 2]), kx, ky)
-
-        def placed(ref, f, c):
-            for n in range(held.shape[0]):
-                for side in range(2):
-                    for h in range(2):
-                        held[n, pl.ds(side + 2 * h, 8, stride=4), :] = ref[
-                            side, 0, h, f, c, :, n * 128 : (n + 1) * 128
-                        ]
-            found = [jnp.where(inside, held[n], 0.0) for n in range(held.shape[0])]
-            count = low // 128
-            between = [jnp.zeros((step, grid_size - 2 * low), jnp.float32)] if 2 * low < grid_size else []
-            return jnp.concatenate(found[:count] + between + found[count:], axis=1)
-
-        is_first = at_ref[0] == 0
-        start = tuple(tuple(i_ref[f, c] for c in range(2)) for f in range(3))
-        before = tuple(tuple(jnp.where(is_first, i_ref[f, c], p_ref[f, c]) for c in range(2)) for f in range(3))
-        new, end = moved(start, 0), moved(before, 1)
-        for f in range(3):
-            for c in range(2):
-                new_ref[0, f, c] = new[f][c] + placed(sum_ref, f, c)
-                res_ref[0, f, c] = (end[f][c] + placed(off_ref, f, c)) - c_ref[0, f, c]
-
-    whole = pl.BlockSpec((1, 3, 2, step, grid_size), lambda i: (0, 0, 0, i, 0))
-    part = pl.BlockSpec((3, 2, step, grid_size), lambda i: (0, 0, i, 0))
-    factor = pl.BlockSpec((2, 3, step, grid_size), lambda i: (0, 0, i, 0))
-    extra = pl.BlockSpec((2, 1, 2, 3, 2, 8, 2 * low), lambda i: (0, i, 0, 0, 0, 0, 0))
-    return pl.pallas_call(
-        kernel,
-        grid=(each,),
-        in_specs=[pl.BlockSpec(memory_space=pltpu.SMEM), whole, part, part, factor, extra, extra],
-        out_specs=[whole, whole],
-        out_shape=[jax.ShapeDtypeStruct(c_state.shape, jnp.float32)] * 2,
-        scratch_shapes=[pltpu.VMEM((2 * low // 128, step, 128), jnp.float32)],
-        name="finish",
-    )(scalars(slab, zone), c_state, init, prev, wide, sums, off)
-
-
 def shards(c_state, init):
-    rows, grid_size = c_state.shape[3:]
     group = lax.axis_size(SPACE)
     slabs = lax.axis_size(SLAB)
     where = (group // 2 - 1, group // 2)
-    off, sums, prev, wide = fine_steps(c_state, init, slabs, group, where)
-    wide = wide.reshape(2, 3, rows, grid_size)
-    return tuple(
-        finish(c_state, init, prev, wide, sums, off, lax.axis_index(SLAB), lax.axis_index(SPACE))
-    )
+    return tuple(fine_steps(c_state, init, slabs, group, where)[:2])
 
 
 def solution(mesh):

time: 218 us -> 203 us (0.931)
  Pallas kernels: 216 us -> 196 us
  local copies, waits for them, and re-layouts: 0 us -> 5.79 us
    pallas_call x1 -> x0, Pallas kernels: 10.8 us -> none  [finish(): pl.pallas_call(kernel, grid=(each,), in_specs=[pl.BlockSpec(memory_space=...]
    pallas_call x1, Pallas kernels: 205 us -> 196 us  [fine_steps(): pl.pallas_call(kernel, in_specs=[pl.BlockSpec(memory_space=pl.ANY)] * 2 +...]
    unnamed x0 -> x4, local copies, waits for them, and re-layouts: none -> 5.79 us
where the time goes in v3:
time: 203 us
  Pallas kernels  196 us (97%)
  local copies, waits for them, and re-layouts  5.79 us (3%)
    pallas_call x1, Pallas kernels, fine_steps(): pl.pallas_call(kernel, in_specs=[pl.BlockSpec(memory_space=pl.ANY)] * 2 +...  196 us
    unnamed x4, local copies, waits for them, and re-layouts  5.79 us

profile of v3, /device:TPU:14, one launch (start us, length us, event | category | flops | bytes accessed | tf_op | source)
XLA Modules:
  0.0 202.7 jit_solution(17873569514913565121)
XLA Ops:
  0.6 196.3 %fine_steps.1 = (f32[1,3,2,128,1024]{4,3,2,1,0:T(8,128)}, f32[1,3,2,128,1024]{4,3,2,1,0:T(8,128)}, f32[3,2,128,1024]{3,2,1,0:T(8,128)}) custom-call(f32[1,3,2,128,1024]{4,3,2,1,0:T(8,128)} %refs_0_.1, f32[3,2,128,1024]{3,2,1,0:T(8,128)} %refs_1_.1, bf16[2,256,256]{2,1,0:T(8,128)(2,1)} %constant.8.clone.refs_2_, f32[2,8,128]{2,1,0:T(8,128)} %constant.9.clone.refs_3_, ...), custom_call_target="tpu_custom_call" | custom-call | tf_op jit(solution)/shard_map/fine_steps/pallas_call | solution.py:817
  196.9 0.0 copy-start
  196.9 4.1 %copy.10 = f32[1,3,2,128,1024]{4,3,2,1,0:T(8,128)} copy(f32[1,3,2,128,1024]{4,3,2,1,0:T(8,128)} %get-tuple-element.8) | data formatting | bytes 6291456
  201.0 0.0 copy-done
  201.0 1.7 copy.11
Async XLA Ops:
  196.9 4.1 %copy-start = (f32[1,3,2,128,1024]{4,3,2,1,0:T(8,128)S(1)}, f32[1,3,2,128,1024]{4,3,2,1,0:T(8,128)}, u32[]{:S(2)}) copy-start(f32[1,3,2,128,1024]{4,3,2,1,0:T(8,128)} %get-tuple-element.9) | copy-start | bytes 9437188

commit v4 on v3

--- a/solution.py
+++ b/solution.py
@@ -130,9 +130,9 @@
     def kernel(*refs):
         c_ref, i_ref, ix, itw, fx, ftw, new_out, res_out, prev = refs[:9]
         state, fields, modes, delta, off, mates, carry_in, sums = refs[9:17]
-        fac, sfac, ie, io, fe, fo, held, dealt = refs[17:25]
-        load, vsend, vrecv, gsend, grecv, bases = refs[25:31]
-        fsend, frecv, msend, mrecv, bsend, brecv, psend, precv, csend, crecv, ssend, osem = refs[31:]
+        fac, sfac, ie, io, fe, fo, held, dealt, winds = refs[17:26]
+        load, vsend, vrecv, gsend, grecv, bases = refs[26:32]
+        fsend, frecv, msend, mrecv, bsend, brecv, psend, precv, csend, crecv, ssend, osem = refs[32:]
         ta, me, z = (lax.axis_index(name) for name in EVERY)
         mate = (ta, 1 - me, z)
         which = jnp.where(z == where[1], 1, 0)
@@ -148,6 +148,7 @@
         kx = jnp.where(kx < grid_size // 2, kx, kx - grid_size).astype(jnp.float32)
         kx_low = jnp.concatenate([kx[:, :low], kx[:, grid_size - low :]], axis=1)
         slots = (2 * me, 2 - me)
+        seat = (0, 1, 3, 2)
 
         barrier = pltpu.get_barrier_semaphore()
         pl.semaphore_signal(barrier, inc=1, device_id=mate, device_id_type=MESH)
@@ -344,7 +345,7 @@
             return home_is_own & (i // each == z)
 
         def field_copy(f, h):
-            lane = slice(f * lanes, (f + 1) * lanes)
+            lane = slice(seat[f] * lanes, (seat[f] + 1) * lanes)
             return pltpu.make_async_remote_copy(
                 fields.at[2, :, h, :, :, lane],
                 fields.at[me, :, h, :, :, lane],
@@ -354,12 +355,13 @@
                 device_id_type=MESH,
             )
 
-        def mode_copy(j):
+        def mode_copy(j, part):
+            lane = slice(0, 3 * lanes) if part == 0 else slice(3 * lanes, 5 * lanes)
             return pltpu.make_async_remote_copy(
-                modes.at[2, j],
-                modes.at[me, j],
-                msend.at[j],
-                mrecv.at[j],
+                modes.at[2, j, :, :, :, lane],
+                modes.at[me, j, :, :, :, lane],
+                msend.at[j, part],
+                mrecv.at[j, part],
                 device_id=mate,
                 device_id_type=pl.DeviceIdType.MESH,
             )
@@ -391,54 +393,73 @@
                 made = dot3(split_pair(jnp.concatenate(turned, axis=0)), (ix[0], ix[1]))
                 for k in range(RADIX):
                     for c in range(2):
-                        fields[slots[k // half], k % half, h, c, row, f * lanes : (f + 1) * lanes] = made[
+                        fields[
+                            slots[k // half], k % half, h, c, row, seat[f] * lanes : (seat[f] + 1) * lanes
+                        ] = made[
                             k * ROWS : (k + 1) * ROWS, c * lanes : (c + 1) * lanes
                         ]
                 return carry
 
             return body
 
-        def middle(j, carry):
-            def rows(c, h):
-                return fields[c, j, h].reshape(2 * per, 4 * lanes)
-
-            even = dot3((ie[0, 0], ie[0, 1]), split_pair(rows(0, 0)))
-            other = dot3((ie[1, 0], ie[1, 1]), split_pair(rows(0, 1)))
-            odd = dot3(
-                (io[0], io[1]), split_pair(jnp.concatenate([rows(1, 0), rows(1, 1)], axis=0))
-            )
-            re, im = odd[: 2 * per], odd[2 * per :]
-            plus, minus = even + other, even - other
-            made = []
-            for grid in (plus + re, minus - im, plus - re, minus + im):
-                u, v, h, w = (grid[:, f * lanes : (f + 1) * lanes] for f in range(4))
-                made.append(
-                    jnp.concatenate([w * v, w * u, 0.5 * (u * u + v * v), h * u, h * v], axis=1)
+        def middle(part):
+            lane = (slice(0, 3 * lanes), slice(3 * lanes, 4 * lanes), slice(0, 4 * lanes))[part]
+            to = (slice(0, 3 * lanes), slice(3 * lanes, 5 * lanes), slice(0, 5 * lanes))[part]
+            width = to.stop - to.start
+
+            def body(j, carry):
+                def side(c, h):
+                    return fields[c, j, h, :, :, lane].reshape(2 * per, lane.stop - lane.start)
+
+                even = dot3((ie[0, 0], ie[0, 1]), split_pair(side(0, 0)))
+                other = dot3((ie[1, 0], ie[1, 1]), split_pair(side(0, 1)))
+                odd = dot3(
+                    (io[0], io[1]), split_pair(jnp.concatenate([side(1, 0), side(1, 1)], axis=0))
                 )
-            a, b = made[0] + made[2], made[1] + made[3]
-            for h, term in enumerate((a + b, a - b)):
-                got = dot3((fe[h, 0], fe[h, 1]), split_pair(term))
-                modes[slots[0], j, h] = got.reshape(2, kept, 5 * lanes)
-            term = jnp.concatenate([made[0] - made[2], made[1] - made[3]], axis=0)
-            got = dot3((fo[0], fo[1]), split_pair(term))
-            for h in range(2):
-                modes[slots[1], j, h] = got[2 * kept * h : 2 * kept * (h + 1)].reshape(
-                    2, kept, 5 * lanes
-                )
-            mode_copy(j).start()
-            return carry
-
-        def read(ref, at):
+                re, im = odd[: 2 * per], odd[2 * per :]
+                plus, minus = even + other, even - other
+                made = []
+                for n, grid in enumerate((plus + re, minus - im, plus - re, minus + im)):
+                    parts = [grid[:, f : f + lanes] for f in range(0, grid.shape[1], lanes)]
+                    products = []
+                    if part == 1:
+                        u, v = winds[j, n, :, :lanes], winds[j, n, :, lanes:]
+                    else:
+                        u, v, w = parts[:3]
+                        products += [w * v, w * u, 0.5 * (u * u + v * v)]
+                    if part == 0:
+                        winds[j, n] = grid[:, : 2 * lanes]
+                    else:
+                        products += [parts[-1] * u, parts[-1] * v]
+                    made.append(jnp.concatenate(products, axis=1))
+                a, b = made[0] + made[2], made[1] + made[3]
+                for h, term in enumerate((a + b, a - b)):
+                    got = dot3((fe[h, 0], fe[h, 1]), split_pair(term))
+                    modes[slots[0], j, h, :, :, to] = got.reshape(2, kept, width)
+                term = jnp.concatenate([made[0] - made[2], made[1] - made[3]], axis=0)
+                got = dot3((fo[0], fo[1]), split_pair(term))
+                for h in range(2):
+                    modes[slots[1], j, h, :, :, to] = got[2 * kept * h : 2 * kept * (h + 1)].reshape(
+                        2, kept, width
+                    )
+                for n in (0, 1):
+                    if part in (n, 2):
+                        mode_copy(j, n).start()
+                return carry
+
+            return body
+
+        def read(ref, at, count=3):
             return tuple(
                 tuple(
                     jnp.concatenate([ref[h, f, c, pl.ds(at, 8)] for h in range(2)], axis=0)
                     for c in range(2)
                 )
-                for f in range(3)
+                for f in range(count)
             )
 
         def write(ref, at, values):
-            for f in range(3):
+            for f in range(len(values)):
                 for c in range(2):
                     for h in range(2):
                         ref[h, f, c, pl.ds(at, 8)] = values[f][c][8 * h : 8 * h + 8]
@@ -464,7 +485,9 @@
             late = lax.rem(m + others, others) * each + last + m // others
             return jnp.where(m < 0, early, late)
 
-        def forward(step):
+        def forward(step, part):
+            which_fields = ((0, 1, 2), (3, 4), (0, 1, 2, 3, 4))[part]
+
             def body(n, carry):
                 i = n if step == 0 else turn_of(n)
                 at, ky, factors = rows_of(i)
@@ -481,14 +504,14 @@
                 stacked = jnp.concatenate(
                     [
                         jnp.concatenate([piece(f, 0, k), piece(f, 1, k)], axis=1)
-                        for f in range(5)
+                        for f in which_fields
                         for k in range(RADIX)
                     ],
                     axis=0,
                 )
                 made = dot3(split_pair(stacked), (fx[0], fx[1]))
                 found = []
-                for f in range(5):
+                for f in range(len(which_fields)):
                     parts = []
                     for k in range(RADIX):
                         start = (f * RADIX + k) * 16
@@ -502,17 +525,24 @@
                     found.append(
                         tuple(jnp.concatenate([p[c] for p in parts], axis=1) for c in range(2))
                     )
-                (ar, ai), (br, bi), (kr, ki), (pr, pi), (qr, qi) = found
                 inside = (jnp.abs(kx) <= limit) & (ky <= limit)
 
                 def keep(values):
                     return jnp.where(inside, dt * values, 0.0)
 
-                change = (
-                    (keep(ar + kx * ki), keep(ai - kx * kr)),
-                    (keep(ky * ki - br), -keep(bi + ky * kr)),
-                    (keep(kx * pi + ky * qi), -keep(kx * pr + ky * qr)),
-                )
+                if part == 1:
+                    change = read(delta, at, 2)
+                else:
+                    (ar, ai), (br, bi), (kr, ki) = found[:3]
+                    change = (
+                        (keep(ar + kx * ki), keep(ai - kx * kr)),
+                        (keep(ky * ki - br), -keep(bi + ky * kr)),
+                    )
+                if part == 0:
+                    write(delta, at, change)
+                    return carry
+                (pr, pi), (qr, qi) = found[-2:]
+                change = (*change, (keep(kx * pi + ky * qi), -keep(kx * pr + ky * qr)))
 
                 def add(left, right):
                     return tuple(tuple(a + b for a, b in zip(p, q)) for p, q in zip(left, right))
@@ -562,24 +592,49 @@
                 fillers[n]()
 
         def steps():
-            for step in range(CF):
+            def columns(f):
+                for h in range(2):
+                    lax.fori_loop(0, blocks, inverse(f, h), 0, unroll=True)
+                    field_copy(f, h).start()
+
+            def columns_wait(f):
+                for h in range(2):
+                    field_copy(f, h).wait()
+
+            def modes_wait(part):
+                for j in range(half):
+                    mode_copy(j, part).wait()
+
+            def arrived(f):
+                for n in (2 * f, 2 * f + 1):
+                    for at in range(group):
+                        gather_wait(n, at)
+
+            for f in (0, 1):
+                arrived(f)
+                columns(f)
+            columns(3)
+            for f in (0, 1, 3):
+                columns_wait(f)
+            lax.fori_loop(0, half, middle(0), 0)
+            modes_wait(0)
+            lax.fori_loop(0, kept // 8, forward(0, 0), 0)
+            arrived(2)
+            columns(2)
+            columns_wait(2)
+            lax.fori_loop(0, half, middle(1), 0)
+            lax.fori_loop(kept // 8, per // 8, plain, 0)
+            modes_wait(1)
+            lax.fori_loop(0, kept // 8, forward(0, 1), 0)
+            for step in range(1, CF):
                 for f in (0, 1, 3, 2):
-                    if step == 0 and f < 3:
-                        for n in (2 * f, 2 * f + 1):
-                            for at in range(group):
-                                gather_wait(n, at)
-                    for h in range(2):
-                        lax.fori_loop(0, blocks, inverse(f, h), 0, unroll=True)
-                        field_copy(f, h).start()
-                for f in range(4):
-                    for h in range(2):
-                        field_copy(f, h).wait()
-                lax.fori_loop(0, half, middle, 0)
-                if step < CF - 1:
-                    lax.fori_loop(kept // 8, per // 8, plain, 0)
-                for j in range(half):
-                    mode_copy(j).wait()
-                lax.fori_loop(0, kept // 8, forward(step), 0)
+                    columns(f)
+                for f in (0, 1, 3, 2):
+                    columns_wait(f)
+                lax.fori_loop(0, half, middle(2), 0)
+                modes_wait(0)
+                modes_wait(1)
+                lax.fori_loop(0, kept // 8, forward(step, 2), 0)
 
         pl.when(is_job)(steps)
 
@@ -834,6 +889,7 @@
             pltpu.VMEM((2, 4 * kept, 2 * quarter), jnp.bfloat16),
             pltpu.VMEM((2, grid_size // 128, rows, 128), jnp.float32),
             pltpu.VMEM((6, 2, 2, short, grid_size), jnp.float32),
+            pltpu.VMEM((half, 4, quarter, 2 * lanes), jnp.float32),
             pltpu.SemaphoreType.DMA((2, grid_size // 128)),
             pltpu.SemaphoreType.DMA((6,)),
             pltpu.SemaphoreType.DMA((6,)),
@@ -842,14 +898,14 @@
             pltpu.SemaphoreType.DMA((3,)),
             pltpu.SemaphoreType.DMA((4, 2)),
             pltpu.SemaphoreType.DMA((4, 2)),
-            pltpu.SemaphoreType.DMA((half,)),
-            pltpu.SemaphoreType.DMA((half,)),
+            pltpu.SemaphoreType.DMA((half, 2)),
+            pltpu.SemaphoreType.DMA((half, 2)),
             pltpu.SemaphoreType.DMA((total, 2)),
             *[pltpu.SemaphoreType.DMA((2, each, 2))] * 6,
             pltpu.SemaphoreType.DMA((2, each)),
         ],
         compiler_params=pltpu.CompilerParams(
-            collective_id=0, has_side_effects=True, vmem_limit_bytes=63 * 1024 * 1024
+            collective_id=0, has_side_effects=True, vmem_limit_bytes=67043328
         ),
         name="fine_steps",
     )(c_state, init, inv_x, inv_tw, fwd_x, fwd_tw)

time: 203 us -> 200 us (0.985); the launches traced: 203 us -> 197 us
  Pallas kernels: 196 us -> 191 us
    pallas_call x1, Pallas kernels: 196 us -> 191 us  [fine_steps(): pl.pallas_call(kernel, in_specs=[pl.BlockSpec(memory_space=pl.ANY)] * 2 +...]
where the time goes in v4:
time: 200 us; the launch traced here: 197 us
  Pallas kernels  191 us (96%)
  local copies, waits for them, and re-layouts  5.79 us (3%)
    pallas_call x1, Pallas kernels, fine_steps(): pl.pallas_call(kernel, in_specs=[pl.BlockSpec(memory_space=pl.ANY)] * 2 +...  191 us
    unnamed x4, local copies, waits for them, and re-layouts  5.79 us

profile of v4, /device:TPU:14, one launch (start us, length us, event | category | flops | bytes accessed | tf_op | source)
XLA Modules:
  0.0 197.2 jit_solution(5532361955066362093)
XLA Ops:
  0.6 190.7 %fine_steps.1 = (f32[1,3,2,128,1024]{4,3,2,1,0:T(8,128)}, f32[1,3,2,128,1024]{4,3,2,1,0:T(8,128)}, f32[3,2,128,1024]{3,2,1,0:T(8,128)}) custom-call(f32[1,3,2,128,1024]{4,3,2,1,0:T(8,128)} %refs_0_.1, f32[3,2,128,1024]{3,2,1,0:T(8,128)} %refs_1_.1, bf16[2,256,256]{2,1,0:T(8,128)(2,1)} %constant.8.clone.refs_2_, f32[2,8,128]{2,1,0:T(8,128)} %constant.9.clone.refs_3_, ...), custom_call_target="tpu_custom_call" | custom-call | tf_op jit(solution)/shard_map/fine_steps/pallas_call | solution.py:872
  191.4 0.0 copy-start
  191.4 4.1 %copy.10 = f32[1,3,2,128,1024]{4,3,2,1,0:T(8,128)} copy(f32[1,3,2,128,1024]{4,3,2,1,0:T(8,128)} %get-tuple-element.8) | data formatting | bytes 6291456
  195.5 0.0 copy-done
  195.5 1.7 copy.11
Async XLA Ops:
  191.4 4.1 %copy-start = (f32[1,3,2,128,1024]{4,3,2,1,0:T(8,128)S(1)}, f32[1,3,2,128,1024]{4,3,2,1,0:T(8,128)}, u32[]{:S(2)}) copy-start(f32[1,3,2,128,1024]{4,3,2,1,0:T(8,128)} %get-tuple-element.9) | copy-start | bytes 9437188
